TPU v7x, 128 devices: a whole 4x4x4 slice. The times are simulated.
128 devices in a mesh: dp: 32 (over y, x, core), tensor: 4 (over z).
Axes of the slice: x: 4, y: 4, z: 4, core: 2. Of those that a mesh axis runs over, the one named last changes fastest.
Arguments:
- tokens: bfloat16 [20480, 1152], P(('dp', 'tensor')), may hold values from -6 to 6
- cotangent: bfloat16 [20480, 1152], P(('dp', 'tensor')), may hold values from -24 to 24
- segment_ids: int32 [32, 640], P('dp'), may hold values from 0 to 3, as said below
- positions: int32 [32, 640], P('dp'), may hold values from 0 to 1999, as said below
- w_query: bfloat16 [1152, 1024], P('dp', 'tensor')
- w_key: bfloat16 [1152, 256], P('dp')
- w_value: bfloat16 [1152, 256], P('dp'), may hold values from -0.1875 to 0.1875
- w_out: bfloat16 [1024, 1152], P('tensor', 'dp'), may hold values from -0.1875 to 0.1875
- w_gate: bfloat16 [1152, 6912], P('dp', 'tensor'), may hold values from -0.1875 to 0.1875
- w_up: bfloat16 [1152, 6912], P('dp', 'tensor'), may hold values from -0.1875 to 0.1875
- w_down: bfloat16 [6912, 1152], P('tensor', 'dp'), may hold values from -0.078125 to 0.078125
- prenorm_attn: bfloat16 [1152], P('dp'), may hold values from 0.099609375 to 1.8984375
- postnorm_attn: bfloat16 [1152], P('dp'), may hold values from 0.099609375 to 1.8984375
- prenorm_ffw: bfloat16 [1152], P('dp'), may hold values from 0.099609375 to 1.8984375
- postnorm_ffw: bfloat16 [1152], P('dp'), may hold values from 0.099609375 to 1.8984375
- query_norm: bfloat16 [256], P('dp'), may hold values from 0.6 to 5
- key_norm: bfloat16 [256], P('dp'), may hold values from 0.6 to 5
Outputs:
- layer_out: bfloat16 [20480, 1152], P(('dp', 'tensor'))
- grad_tokens: float32 [20480, 1152], P(('dp', 'tensor'))
- grad_query: float32 [1152, 1024], P('dp', 'tensor')
- grad_key: float32 [1152, 256], P('dp')
- grad_value: float32 [1152, 256], P('dp')
- grad_output: float32 [1024, 1152], P('tensor', 'dp')
- grad_gate: float32 [1152, 6912], P('dp', 'tensor')
- grad_up: float32 [1152, 6912], P('dp', 'tensor')
- grad_down: float32 [6912, 1152], P('tensor', 'dp')
- grad_prenorm_attn: float32 [1152], P('dp')
- grad_postnorm_attn: float32 [1152], P('dp')
- grad_prenorm_ffw: float32 [1152], P('dp')
- grad_postnorm_ffw: float32 [1152], P('dp')
- grad_query_norm: float32 [256], P('dp')
- grad_key_norm: float32 [256], P('dp')
Inputs may be any that keep to these rules, and one draw needn't show every extreme that they name: `segment_ids`: within each sequence the numbers never fall; a document is a run of equal numbers. Within a document positions rise by one from token to token.
All inputs are finite; a program needn't handle non-finite values.
Results may differ from a plain program's by a relative error of at most 0.033.
The roundings to bfloat16 on the way count: a program that leaves them out, or rounds other values in their place, can miss the bound.
Values may be sent and summed in bfloat16 or wider, within the bound.
A program may use at most 128 MiB of HBM per device.

v0:
```python
import math

import jax
import jax.numpy as jnp
from jax import lax
from jax.sharding import PartitionSpec as P

WINDOW = 512


EPSILON = 1e-06
ROPE_BASE = 10000.0
GELU_SCALE = math.sqrt(2.0 / math.pi)
MASKED = -1e30


def normalize(inputs):
    inverse = lax.rsqrt(jnp.mean(inputs * inputs, axis=-1, keepdims=True) + EPSILON)
    return (inputs * inverse, inverse)


def normalize_back(grad_hat, normed, inverse):
    return inverse * (grad_hat - normed * jnp.mean(grad_hat * normed, axis=-1, keepdims=True))


def rotary_tables(places, width):
    half = width // 2
    freqs = ROPE_BASE ** (-(jnp.arange(half, dtype=jnp.float32) * 2.0) / width)
    angles = places.astype(jnp.float32)[:, None] * freqs[None, :]
    return (jnp.cos(angles), jnp.sin(angles))


def rotate(inputs, cosine, sine):
    half = inputs.shape[-1] // 2
    first = inputs[:, :half]
    second = inputs[:, half:]
    return jnp.concatenate(
        [first * cosine - second * sine, second * cosine + first * sine], axis=-1
    )


def gelu_parts(inputs):
    inner = GELU_SCALE * (inputs + 0.044715 * inputs * inputs * inputs)
    tangent = jnp.tanh(inner)
    result = 0.5 * inputs * (1.0 + tangent)
    slope = 0.5 * (1.0 + tangent) + 0.5 * inputs * (1.0 - tangent * tangent) * GELU_SCALE * (
        1.0 + 3.0 * 0.044715 * inputs * inputs
    )
    return (result, slope)


def window_mask(segments):
    length = segments.shape[0]
    places = jnp.arange(length, dtype=jnp.int32)
    offset = places[:, None] - places[None, :]
    same = segments[:, None] == segments[None, :]
    return same & (offset >= 0) & (offset < WINDOW)


def contract_rows(left, right):
    return lax.dot_general(
        left, right, (((0,), (0,)), ((), ())), preferred_element_type=jnp.float32
    )


def contract_cols(left, right):
    return lax.dot_general(
        left, right, (((1,), (1,)), ((), ())), preferred_element_type=jnp.float32
    )


def attend_scores(queries, keys, allowed, scale):
    return jnp.where(allowed, contract_cols(queries, keys) * scale, MASKED)


def attend_forward(queries, keys, values, allowed, scale):
    scores = attend_scores(queries, keys, allowed, scale)
    top = jnp.max(scores, axis=-1, keepdims=True)
    totals = jnp.sum(jnp.exp(scores - top), axis=-1, keepdims=True)
    logsum = top + jnp.log(totals)
    probs = jnp.exp(scores - logsum).astype(jnp.bfloat16)
    return (jnp.dot(probs, values, preferred_element_type=jnp.float32), logsum)


def attend_backward(queries, keys, values, allowed, scale, logsum, grad_heads):
    probs = jnp.exp(attend_scores(queries, keys, allowed, scale) - logsum)
    grad_values = contract_rows(probs.astype(jnp.bfloat16), grad_heads)
    grad_probs = contract_cols(grad_heads, values)
    centre = jnp.sum(probs * grad_probs, axis=-1, keepdims=True)
    grad_scores = (probs * (grad_probs - centre) * scale).astype(jnp.bfloat16)
    grad_queries = jnp.dot(grad_scores, keys, preferred_element_type=jnp.float32)
    grad_keys = contract_rows(grad_scores, queries)
    return (grad_queries, grad_keys, grad_values)


def local(
    tokens,
    cotangent,
    segment_ids,
    positions,
    w_query,
    w_key,
    w_value,
    w_out,
    w_gate,
    w_up,
    w_down,
    prenorm_attn,
    postnorm_attn,
    prenorm_ffw,
    postnorm_ffw,
    query_norm,
    key_norm,
):
    residual = tokens.astype(jnp.float32)
    attn_mats = (
        lax.all_gather(w_query, "dp", axis=0, tiled=True),
        lax.all_gather(w_key, "dp", axis=0, tiled=True),
        lax.all_gather(w_value, "dp", axis=0, tiled=True),
        lax.all_gather(w_out, "dp", axis=1, tiled=True),
        lax.all_gather(prenorm_attn, "dp", axis=0, tiled=True),
        lax.all_gather(postnorm_attn, "dp", axis=0, tiled=True),
        lax.all_gather(query_norm, "dp", axis=0, tiled=True),
        lax.all_gather(key_norm, "dp", axis=0, tiled=True),
    )
    full_query, full_key, full_value, full_out = (
        attn_mats[0],
        attn_mats[1],
        attn_mats[2],
        attn_mats[3],
    )
    gain_in = attn_mats[4].astype(jnp.float32)
    gain_post = attn_mats[5].astype(jnp.float32)
    gain_query = attn_mats[6].astype(jnp.float32)
    gain_key = attn_mats[7].astype(jnp.float32)
    normed_in, inverse_in = normalize(residual)
    attn_rows = lax.all_gather(
        (normed_in * gain_in).astype(jnp.bfloat16), "tensor", axis=0, tiled=True
    )
    width = full_key.shape[1]
    scale = 1.0 / math.sqrt(width)
    cosine, sine = rotary_tables(positions.reshape(-1), width)
    masks = [window_mask(segment_ids[0])]
    key_hat, key_inverse = normalize(
        jnp.dot(attn_rows, full_key, preferred_element_type=jnp.float32)
    )
    keys = rotate(key_hat * gain_key, cosine, sine).astype(jnp.bfloat16)
    values = jnp.dot(attn_rows, full_value, preferred_element_type=jnp.float32).astype(jnp.bfloat16)
    query_hat, query_inverse = normalize(
        jnp.dot(attn_rows, full_query, preferred_element_type=jnp.float32)
    )
    queries = rotate(query_hat * gain_query, cosine, sine).astype(jnp.bfloat16)
    sequence = 0
    piece, logsum = attend_forward(queries, keys, values, masks[sequence], scale)
    logsums = logsum
    saved = [(query_hat, query_inverse, queries, logsums)]
    heads_out = piece.astype(jnp.bfloat16)
    attn_sum = lax.psum_scatter(
        jnp.dot(heads_out, full_out, preferred_element_type=jnp.float32),
        "tensor",
        scatter_dimension=0,
        tiled=True,
    )
    attn_hat, attn_inverse = normalize(attn_sum)
    hidden = residual + attn_hat * gain_post
    ffw_mats = (
        lax.all_gather(w_gate, "dp", axis=0, tiled=True),
        lax.all_gather(w_up, "dp", axis=0, tiled=True),
        lax.all_gather(w_down, "dp", axis=1, tiled=True),
        lax.all_gather(prenorm_ffw, "dp", axis=0, tiled=True),
        lax.all_gather(postnorm_ffw, "dp", axis=0, tiled=True),
    )
    full_gate, full_up, full_down = (ffw_mats[0], ffw_mats[1], ffw_mats[2])
    gain_ffw_in = ffw_mats[3].astype(jnp.float32)
    gain_ffw_post = ffw_mats[4].astype(jnp.float32)
    mid_hat, mid_inverse = normalize(hidden)
    ffw_rows = lax.all_gather(
        (mid_hat * gain_ffw_in).astype(jnp.bfloat16), "tensor", axis=0, tiled=True
    )
    gate = jnp.dot(ffw_rows, full_gate, preferred_element_type=jnp.float32)
    upward = jnp.dot(ffw_rows, full_up, preferred_element_type=jnp.float32)
    gelu_value, gelu_slope = gelu_parts(gate)
    act = (gelu_value * upward).astype(jnp.bfloat16)
    ffw_sum = lax.psum_scatter(
        jnp.dot(act, full_down, preferred_element_type=jnp.float32),
        "tensor",
        scatter_dimension=0,
        tiled=True,
    )
    ffw_hat, ffw_inverse = normalize(ffw_sum)
    layer_out = (hidden + ffw_hat * gain_ffw_post).astype(jnp.bfloat16)
    back_mats = (
        lax.all_gather(w_query, "dp", axis=0, tiled=True),
        lax.all_gather(w_key, "dp", axis=0, tiled=True),
        lax.all_gather(w_value, "dp", axis=0, tiled=True),
        lax.all_gather(w_out, "dp", axis=1, tiled=True),
        lax.all_gather(w_gate, "dp", axis=0, tiled=True),
        lax.all_gather(w_up, "dp", axis=0, tiled=True),
        lax.all_gather(w_down, "dp", axis=1, tiled=True),
    )
    back_query, back_key, back_value, back_out = (
        back_mats[0],
        back_mats[1],
        back_mats[2],
        back_mats[3],
    )
    back_gate, back_up, back_down = (back_mats[4], back_mats[5], back_mats[6])
    grad_out = cotangent.astype(jnp.float32)
    grad_post_ffw = jnp.sum(grad_out * ffw_hat, axis=0)
    grad_ffw_local = normalize_back(grad_out * gain_ffw_post, ffw_hat, ffw_inverse).astype(
        jnp.bfloat16
    )
    grad_ffw = lax.all_gather(grad_ffw_local, "tensor", axis=0, tiled=True)
    grad_down_turned = contract_rows(grad_ffw, act)
    grad_act = contract_cols(grad_ffw, back_down)
    grad_gate_in = (grad_act * upward * gelu_slope).astype(jnp.bfloat16)
    grad_up_in = (grad_act * gelu_value).astype(jnp.bfloat16)
    grad_gate = contract_rows(ffw_rows, grad_gate_in)
    grad_up = contract_rows(ffw_rows, grad_up_in)
    ffw_in_shards = (
        lax.psum_scatter(
            grad_gate.astype(jnp.bfloat16), "dp", scatter_dimension=0, tiled=True
        ).astype(jnp.float32),
        lax.psum_scatter(
            grad_up.astype(jnp.bfloat16), "dp", scatter_dimension=0, tiled=True
        ).astype(jnp.float32),
    )
    grad_mid = lax.psum_scatter(
        contract_cols(grad_gate_in, back_gate) + contract_cols(grad_up_in, back_up),
        "tensor",
        scatter_dimension=0,
        tiled=True,
    )
    grad_pre_ffw = jnp.sum(grad_mid * mid_hat, axis=0)
    grad_hidden = grad_out + normalize_back(grad_mid * gain_ffw_in, mid_hat, mid_inverse)
    grad_post_attn = jnp.sum(grad_hidden * attn_hat, axis=0)
    grad_attn_local = normalize_back(grad_hidden * gain_post, attn_hat, attn_inverse).astype(
        jnp.bfloat16
    )
    grad_attn = lax.all_gather(grad_attn_local, "tensor", axis=0, tiled=True)
    grad_out_turned = contract_rows(grad_attn, heads_out)
    grad_heads = contract_cols(grad_attn, back_out).astype(jnp.bfloat16)
    which = 0
    query_hat, query_inverse, queries, logsum = saved[which]
    sequence = 0
    grad_queries, grad_keys, grad_values = attend_backward(
        queries, keys, values, masks[sequence], scale, logsum, grad_heads
    )
    grad_query_turned = rotate(grad_queries, cosine, -sine)
    grad_query_norm = jnp.sum(grad_query_turned * query_hat, axis=0)
    query_in = normalize_back(grad_query_turned * gain_query, query_hat, query_inverse).astype(
        jnp.bfloat16
    )
    grad_key_turned = rotate(grad_keys, cosine, -sine)
    grad_key_norm = jnp.sum(grad_key_turned * key_hat, axis=0)
    key_in = normalize_back(grad_key_turned * gain_key, key_hat, key_inverse).astype(jnp.bfloat16)
    value_in = grad_values.astype(jnp.bfloat16)
    query_blocks = contract_rows(attn_rows, query_in)
    grad_key = contract_rows(attn_rows, key_in)
    grad_value = contract_rows(attn_rows, value_in)
    query_ins = [query_in]
    key_ins = [key_in]
    value_ins = [value_in]
    which = 0
    total = contract_cols(query_ins[which], back_query)
    total = total + contract_cols(key_ins[which], back_key)
    total = total + contract_cols(value_ins[which], back_value)
    grad_in_rows = lax.psum_scatter(
        total.astype(jnp.bfloat16), "tensor", scatter_dimension=0, tiled=True
    ).astype(jnp.float32)
    grad_pre_attn = jnp.sum(grad_in_rows * normed_in, axis=0)
    grad_tokens = grad_hidden + normalize_back(grad_in_rows * gain_in, normed_in, inverse_in)
    rest = (
        lax.psum_scatter(
            query_blocks.astype(jnp.bfloat16), "dp", scatter_dimension=0, tiled=True
        ).astype(jnp.float32),
        lax.psum_scatter(
            grad_key.astype(jnp.bfloat16), "dp", scatter_dimension=0, tiled=True
        ).astype(jnp.float32),
        lax.psum_scatter(
            grad_value.astype(jnp.bfloat16), "dp", scatter_dimension=0, tiled=True
        ).astype(jnp.float32),
        lax.psum_scatter(
            grad_out_turned.astype(jnp.bfloat16), "dp", scatter_dimension=0, tiled=True
        ).astype(jnp.float32),
        lax.psum_scatter(
            grad_down_turned.astype(jnp.bfloat16), "dp", scatter_dimension=0, tiled=True
        ).astype(jnp.float32),
        lax.psum_scatter(
            grad_pre_attn.astype(jnp.bfloat16), "dp", scatter_dimension=0, tiled=True
        ).astype(jnp.float32),
        lax.psum_scatter(
            grad_post_attn.astype(jnp.bfloat16), "dp", scatter_dimension=0, tiled=True
        ).astype(jnp.float32),
        lax.psum_scatter(
            grad_pre_ffw.astype(jnp.bfloat16), "dp", scatter_dimension=0, tiled=True
        ).astype(jnp.float32),
        lax.psum_scatter(
            grad_post_ffw.astype(jnp.bfloat16), "dp", scatter_dimension=0, tiled=True
        ).astype(jnp.float32),
        lax.psum_scatter(
            grad_query_norm.astype(jnp.bfloat16), "dp", scatter_dimension=0, tiled=True
        ).astype(jnp.float32),
        lax.psum_scatter(
            grad_key_norm.astype(jnp.bfloat16), "dp", scatter_dimension=0, tiled=True
        ).astype(jnp.float32),
    )
    shared = (
        lax.psum(rest[1].astype(jnp.bfloat16), "tensor").astype(jnp.float32),
        lax.psum(rest[2].astype(jnp.bfloat16), "tensor").astype(jnp.float32),
        lax.psum(rest[5].astype(jnp.bfloat16), "tensor").astype(jnp.float32),
        lax.psum(rest[6].astype(jnp.bfloat16), "tensor").astype(jnp.float32),
        lax.psum(rest[7].astype(jnp.bfloat16), "tensor").astype(jnp.float32),
        lax.psum(rest[8].astype(jnp.bfloat16), "tensor").astype(jnp.float32),
        lax.psum(rest[9].astype(jnp.bfloat16), "tensor").astype(jnp.float32),
        lax.psum(rest[10].astype(jnp.bfloat16), "tensor").astype(jnp.float32),
    )
    return (
        layer_out,
        grad_tokens,
        rest[0],
        shared[0],
        shared[1],
        rest[3].T,
        ffw_in_shards[0],
        ffw_in_shards[1],
        rest[4].T,
        shared[2],
        shared[3],
        shared[4],
        shared[5],
        shared[6],
        shared[7],
    )


def solution(mesh):
    placed = (
        P(("dp", "tensor"), None),
        P(("dp", "tensor"), None),
        P("dp", None),
        P("dp", None),
        P("dp", "tensor"),
        P("dp", None),
        P("dp", None),
        P("tensor", "dp"),
        P("dp", "tensor"),
        P("dp", "tensor"),
        P("tensor", "dp"),
        P("dp"),
        P("dp"),
        P("dp"),
        P("dp"),
        P("dp"),
        P("dp"),
    )
    return jax.shard_map(
        local,
        mesh=mesh,
        in_specs=placed,
        out_specs=(
            P(("dp", "tensor"), None),
            P(("dp", "tensor"), None),
            P("dp", "tensor"),
            P("dp", None),
            P("dp", None),
            P("tensor", "dp"),
            P("dp", "tensor"),
            P("dp", "tensor"),
            P("tensor", "dp"),
            P("dp"),
            P("dp"),
            P("dp"),
            P("dp"),
            P("dp"),
            P("dp"),
        ),
        check_vma=False,
    )
```

profile of v0, /device:TPU:0, one launch (start us, length us, event | category | flops | bytes accessed | tf_op | source)
XLA Modules:
  0.0 971.6 jit_solution(9938166193788936195)
XLA Ops:
  15.8 128.5 %all-reduce.27 = (bf16[1152]{0:T(1024)(128)(2,1)S(1)}, bf16[256]{0:T(256)(128)(2,1)S(1)}, bf16[256]{0:T(256)(128)(2,1)S(1)}, bf16[1152]{0:T(1024)(128)(2,1)S(1)}...) all-reduce(bf16[1152]{0:T(1024)(128)(2,1)S(1)} %dynamic-update-slic, ...), channel_id=1, replica_groups=mesh['dp'=32,'tensor'=4] {'dp'}, use_global_device_ids=true, to_apply=%add | all-reduce | flops 5120 | bytes 20480
  145.5 1.9 fusion.32
  147.5 22.5 %all-gather.2 = bf16[32,36,256]{2,1,0:T(8,128)(2,1)S(1)} all-gather(bf16[1,36,256]{2,1,0:T(8,128)(2,1)} %bitcast.84), channel_id=1, replica_groups=mesh['dp'=32,'tensor'=4] {'dp'}, dimensions={0}, use_global_device_ids=true | all-gather | bytes 608256 | tf_op jit(solution)/shard_map/all_gather | solution.py:119
  170.2 24.3 %all-gather.1 = bf16[32,36,256]{2,1,0:T(8,128)(2,1)S(1)} all-gather(bf16[1,36,256]{2,1,0:T(8,128)(2,1)S(1)} %bitcast.85), channel_id=1, replica_groups=mesh['dp'=32,'tensor'=4] {'dp'}, dimensions={0}, use_global_device_ids=true | all-gather | bytes 608256 | tf_op jit(solution)/shard_map/all_gather | solution.py:118
  194.7 22.6 %all-gather = bf16[32,36,256]{2,1,0:T(8,128)(2,1)S(1)} all-gather(bf16[1,36,256]{2,1,0:T(8,128)(2,1)S(1)} %bitcast.86), channel_id=1, replica_groups=mesh['dp'=32,'tensor'=4] {'dp'}, dimensions={0}, use_global_device_ids=true | all-gather | bytes 608256 | tf_op jit(solution)/shard_map/all_gather | solution.py:117
  217.5 24.6 %all-gather.3 = bf16[32,36,256]{2,1,0:T(8,128)(2,1)S(1)} all-gather(bf16[1,36,256]{2,1,0:T(8,128)(2,1)S(1)} %bitcast.87), channel_id=1, replica_groups=mesh['dp'=32,'tensor'=4] {'dp'}, dimensions={0}, use_global_device_ids=true | all-gather | bytes 608256 | tf_op jit(solution)/shard_map/all_gather | solution.py:120
  242.3 2.3 multiply_reduce_fusion.12
  245.6 1.5 fusion.59
  250.8 2.2 fusion.76
  254.9 34.6 %reduce-scatter.19.cloned.1.call-done = f32[160,1152]{1,0:T(8,128)} async-done(((f32[640,1152]{1,0:T(8,128)}), f32[160,1152]{1,0:T(8,128)}) %reduce-scatter.19.cloned.1.call-update) | async-done | bytes 737296 | tf_op jit(solution)/shard_map/reduce_scatter | solution.py:158
  293.6 8.0 all-gather.23.cloned.1.call-done
  301.6 7.3 reshape.160
  308.9 40.7 %all-gather.25.cloned.1.call-done = bf16[32,36,1728]{2,1,0:T(8,128)(2,1)} async-done(((bf16[1,36,1728]{2,1,0:T(8,128)(2,1)}), bf16[32,36,1728]{2,1,0:T(8,128)(2,1)}) %all-gather.25.cloned.1.call-update) | async-done | bytes 3981328 | tf_op jit(solution)/shard_map/all_gather | solution.py:168
  349.5 7.3 reshape.162
  356.8 40.7 %all-gather.27.cloned.1.call-done = bf16[32,36,1728]{2,1,0:T(8,128)(2,1)} async-done(((bf16[1,36,1728]{2,1,0:T(8,128)(2,1)}), bf16[32,36,1728]{2,1,0:T(8,128)(2,1)}) %all-gather.27.cloned.1.call-update) | async-done | bytes 3981328 | tf_op jit(solution)/shard_map/all_gather | solution.py:169
  397.5 7.3 reshape.164
  404.8 20.2 %all-gather.17.cloned.1.call-done = bf16[640,1152]{1,0:T(8,128)(2,1)} async-done(((bf16[160,1152]{1,0:T(8,128)(2,1)}), bf16[640,1152]{1,0:T(8,128)(2,1)}) %all-gather.17.cloned.1.call-update) | async-done | bytes 1474576 | tf_op jit(solution)/shard_map/all_gather | solution.py:177
  425.0 6.5 fusion.77
  431.5 6.7 multiply_convert_fusion.1
  439.7 4.8 fusion.78
  444.7 36.9 %reduce-scatter.21.cloned.1.call-done = f32[160,1152]{1,0:T(8,128)} async-done(((f32[640,1152]{1,0:T(8,128)}), f32[160,1152]{1,0:T(8,128)}) %reduce-scatter.21.cloned.1.call-update) | async-done | bytes 737296 | tf_op jit(solution)/shard_map/reduce_scatter | solution.py:184
  485.6 25.6 %all-gather.19.cloned.1.call-done = bf16[640,1152]{1,0:T(8,128)(2,1)} async-done(((bf16[160,1152]{1,0:T(8,128)(2,1)}), bf16[640,1152]{1,0:T(8,128)(2,1)}) %all-gather.19.cloned.1.call-update) | async-done | bytes 1474576 | tf_op jit(solution)/shard_map/all_gather | solution.py:213
  511.2 10.2 %multiply_convert_fusion = (bf16[640,1728]{0,1:T(8,128)(2,1)S(1)}, bf16[640,1728]{0,1:T(8,128)(2,1)S(1)}) fusion(f32[640,1728]{0,1:T(8,128)} %copy-done.52, f32[640,1728]{0,1:T(8,128)} %get-tuple-element.90, bf16[640,1152]{1,0:T(8,128)(2,1)} %all-gather.19.cloned.1.call-done, bf16[1152,1728]{1,0:T(8,128)(2,1)} %reshape.164), kind=kOutput, calls=%fused_computation.12 | convolution fusion | flops 2573475840 | bytes 18726912 | tf_op jit(solution)/shard_map/dot_general | solution.py:67
  521.5 3.2 fusion.79
  525.2 4.9 convolution_add_fusion.2
  530.2 37.1 %reduce-scatter.23.cloned.1.call-done = f32[160,1152]{1,0:T(8,128)} async-done(((f32[640,1152]{1,0:T(8,128)}), f32[160,1152]{1,0:T(8,128)}) %reduce-scatter.23.cloned.1.call-update) | async-done | bytes 737296 | tf_op jit(solution)/shard_map/reduce_scatter | solution.py:228
  568.8 1.8 multiply_reduce_fusion.2
  572.7 7.7 convolution_convert_fusion.2
  580.4 5.4 convolution_convert_fusion.1
  585.8 12.3 %all-gather.21.cloned.1.call-done = bf16[640,1152]{1,0:T(8,128)(2,1)} async-done(((bf16[160,1152]{1,0:T(8,128)(2,1)}), bf16[640,1152]{1,0:T(8,128)(2,1)}) %all-gather.21.cloned.1.call-update) | async-done | bytes 1474576 | tf_op jit(solution)/shard_map/all_gather | solution.py:240
  598.0 2.0 convolution_convert_fusion.8
  603.0 1.7 fusion.56
  608.6 1.8 fusion.14
  610.4 7.6 convolution_convert_fusion
  618.7 1.5 convolution_convert_fusion.5
  620.2 1.5 convolution_convert_fusion.4
  623.2 98.4 %fusion.73 = (bf16[40,256]{1,0:T(8,128)(2,1)S(1)}, bf16[40,256]{1,0:T(8,128)(2,1)S(1)}, bf16[40,256]{1,0:T(8,128)(2,1)S(1)}, bf16[40,256]{1,0:T(8,128)(2,1)S(1)}...) fusion(bf16[1152,256]{1,0:T(8,128)(2,1)S(1)} %convolution_convert_fusion.6, ...), kind=kCustom, calls=%all-reduce-scatter.7 | all-reduce-scatter fusion | flops 7946241 | bytes 14800384
  724.3 5.6 collective-permute-start.23
  730.0 2.2 collective-permute-start.3
  732.1 5.3 collective-permute-start.7
  737.5 3.0 collective-permute-start.11
  740.5 5.2 collective-permute-start.15
  747.0 2.1 collective-permute-start
  749.1 5.1 collective-permute-start.6
  754.3 4.0 collective-permute-start.5
  759.8 3.3 collective-permute-start.10
  763.1 3.7 collective-permute-start.9
  766.8 2.5 collective-permute-start.14
  769.4 3.6 collective-permute-start.13
  773.1 2.3 collective-permute-start.12
  778.4 2.5 collective-permute-start.8
  781.0 1.9 collective-permute-start.18
  782.9 2.5 collective-permute-start.17
  785.4 1.7 collective-permute-start.16
  787.1 2.4 collective-permute-start.22
  790.7 2.1 collective-permute-start.21
  794.0 2.5 collective-permute-start.20
  798.0 2.9 collective-permute-start.25
  800.9 2.4 collective-permute-start.24
  806.4 2.5 concatenate.23
  809.4 3.2 concatenate.24
  816.3 123.9 %all-reduce.26 = (bf16[1152]{0:T(1024)(128)(2,1)S(1)}, bf16[1152]{0:T(1024)(128)(2,1)S(1)}, bf16[1152]{0:T(1024)(128)(2,1)S(1)}, bf16[1152]{0:T(1024)(128)(2,1)S...) all-reduce(bf16[1152]{0:T(1024)(128)(2,1)S(1)} %get-tuple-element.2, ...), channel_id=13, replica_groups=mesh['dp'=32,'tensor'=4] {'dp'}, use_global_device_ids=true, to_apply=%region_29.30.clone | all-reduce | flops 5120 | bytes 20480
  940.7 16.3 %all-reduce.28 = (bf16[36,256]{1,0:T(8,128)(2,1)S(1)}, bf16[36,256]{1,0:T(8,128)(2,1)S(1)}, bf16[36]{0:T(256)(128)(2,1)S(1)}, bf16[36]{0:T(256)(128)(2,1)S(1)}, ...) all-reduce(bf16[36,256]{1,0:T(8,128)(2,1)S(1)} %constant_dynamic-sl, ...), channel_id=1, replica_groups=mesh['dp'=32,'tensor'=4] {'tensor'}, use_global_device_ids=true, to_apply=%region_21.22 | all-reduce | flops 18592 | bytes 74368 | tf_op jit(solution)/shard_map/psum | solution.py:309
  961.3 2.2 fusion.31
  (273 shorter events, 59.7 us)
Async XLA Ops:
  8.0 162.2 %copy-start.38 = (bf16[36,256]{1,0:T(8,128)(2,1)S(1)}, bf16[36,256]{1,0:T(8,128)(2,1)}, u32[]{:S(2)}) copy-start(bf16[36,256]{1,0:T(8,128)(2,1)} %param.22) | copy-start | bytes 55300
  8.0 234.3 %all-gather.15.cloned.1.call-start = ((), (), s32[]{:S(2)}) async-start(), calls=%async_computation.4 | async-start | bytes 1843200 | tf_op jit(solution)/shard_map/all_gather | solution.py:137
  147.4 47.3 %copy-start.39 = (bf16[36,256]{1,0:T(8,128)(2,1)S(1)}, bf16[36,256]{1,0:T(8,128)(2,1)}, u32[]{:S(2)}) copy-start(bf16[36,256]{1,0:T(8,128)(2,1)} %param.21) | copy-start | bytes 55300
  147.5 142.0 %reduce-scatter.19.cloned.1.call-start = ((), (), s32[]{:S(2)}) async-start(), calls=%async_computation.5 | async-start | bytes 3686400 | tf_op jit(solution)/shard_map/reduce_scatter | solution.py:158
  170.2 78.1 %copy-start.20 = (bf16[1152,256]{1,0:T(8,128)(2,1)}, bf16[1152,256]{1,0:T(8,128)(2,1)S(1)}, u32[]{:S(2)}) copy-start(bf16[1152,256]{1,0:T(8,128)(2,1)S(1)} %reshape.156) | copy-start | bytes 1769476
  170.2 47.3 %copy-start.40 = (bf16[256,36]{0,1:T(8,128)(2,1)S(1)}, bf16[256,36]{0,1:T(8,128)(2,1)}, u32[]{:S(2)}) copy-start(bf16[256,36]{0,1:T(8,128)(2,1)} %param.24) | copy-start | bytes 55300
  194.6 49.9 %copy-start.11 = (bf16[1152,256]{1,0:T(8,128)(2,1)}, bf16[1152,256]{1,0:T(8,128)(2,1)S(1)}, u32[]{:S(2)}) copy-start(bf16[1152,256]{1,0:T(8,128)(2,1)S(1)} %reshape.154) | copy-start | bytes 1769476
  194.7 47.5 %copy-start.44 = (s32[1,640]{1,0:T(1,128)S(1)}, s32[1,640]{1,0:T(1,128)}, u32[]{:S(2)}) copy-start(s32[1,640]{1,0:T(1,128)} %param.19) | copy-start | bytes 7684
  194.7 47.6 %copy-start.45 = (s32[1,640]{1,0:T(1,128)S(1)}, s32[1,640]{1,0:T(1,128)}, u32[]{:S(2)}) copy-start(s32[1,640]{1,0:T(1,128)} %param.20) | copy-start | bytes 7684
  194.7 50.7 %copy-start.42 = (f32[256]{0:T(256)}, f32[256]{0:T(256)S(1)}, u32[]{:S(2)}) copy-start(f32[256]{0:T(256)S(1)} %convert_element_type.184) | copy-start | bytes 3076
  217.5 27.1 %copy-start.13 = (bf16[1152,256]{1,0:T(8,128)(2,1)}, bf16[1152,256]{1,0:T(8,128)(2,1)S(1)}, u32[]{:S(2)}) copy-start(bf16[1152,256]{1,0:T(8,128)(2,1)S(1)} %reshape.152) | copy-start | bytes 1769476
  242.2 7.9 copy-start.22
  253.0 37.7 %copy-start.5 = (bf16[160,1152]{1,0:T(8,128)(2,1)S(1)}, bf16[160,1152]{1,0:T(8,128)(2,1)}, u32[]{:S(2)}) copy-start(bf16[160,1152]{1,0:T(8,128)(2,1)} %param.17) | copy-start | bytes 1105924
  253.1 48.5 %all-gather.23.cloned.1.call-start = ((), (), s32[]{:S(2)}) async-start(), calls=%async_computation.12 | async-start | bytes 4730880 | tf_op jit(solution)/shard_map/all_gather | solution.py:167
  253.6 95.9 %all-gather.25.cloned.1.call-start = ((), (), s32[]{:S(2)}) async-start(), calls=%async_computation.13 | async-start | bytes 4730880 | tf_op jit(solution)/shard_map/all_gather | solution.py:168
  254.2 143.3 %all-gather.27.cloned.1.call-start = ((), (), s32[]{:S(2)}) async-start(), calls=%async_computation.14 | async-start | bytes 4730880 | tf_op jit(solution)/shard_map/all_gather | solution.py:169
  254.8 170.2 %all-gather.17.cloned.1.call-start = ((), (), s32[]{:S(2)}) async-start(), calls=%async_computation.6 | async-start | bytes 1843200 | tf_op jit(solution)/shard_map/all_gather | solution.py:177
  293.1 188.5 %reduce-scatter.21.cloned.1.call-start = ((), (), s32[]{:S(2)}) async-start(), calls=%async_computation.7 | async-start | bytes 3686400 | tf_op jit(solution)/shard_map/reduce_scatter | solution.py:184
  425.0 6.6 copy-start.16
  425.0 6.6 copy-start.49
  431.5 6.7 copy-start.52
  431.5 8.1 copy-start.18
  444.4 38.5 %copy-start.19 = (bf16[160,1152]{1,0:T(8,128)(2,1)S(1)}, bf16[160,1152]{1,0:T(8,128)(2,1)}, u32[]{:S(2)}) copy-start(bf16[160,1152]{1,0:T(8,128)(2,1)} %param.18) | copy-start | bytes 1105924
  444.5 66.7 %all-gather.19.cloned.1.call-start = ((), (), s32[]{:S(2)}) async-start(), calls=%async_computation.8 | async-start | bytes 1843200 | tf_op jit(solution)/shard_map/all_gather | solution.py:213
  485.6 81.7 %reduce-scatter.23.cloned.1.call-start = ((), (), s32[]{:S(2)}) async-start(), calls=%async_computation.9 | async-start | bytes 3686400 | tf_op jit(solution)/shard_map/reduce_scatter | solution.py:228
  511.2 10.3 %copy-start.15 = (bf16[1152,1728]{1,0:T(8,128)(2,1)S(1)}, bf16[1152,1728]{1,0:T(8,128)(2,1)}, u32[]{:S(2)}) copy-start(bf16[1152,1728]{1,0:T(8,128)(2,1)} %reshape.160) | copy-start | bytes 11943940
  530.2 38.6 %copy-start = (f32[160,1152]{1,0:T(8,128)S(1)}, f32[160,1152]{1,0:T(8,128)}, u32[]{:S(2)}) copy-start(f32[160,1152]{1,0:T(8,128)} %reduce-scatter.19.cloned.1.call-done) | copy-start | bytes 2211844
  530.2 67.8 %all-gather.21.cloned.1.call-start = ((), (), s32[]{:S(2)}) async-start(), calls=%async_computation.10 | async-start | bytes 1843200 | tf_op jit(solution)/shard_map/all_gather | solution.py:240
  572.4 242.5 %reduce-scatter.25.cloned.1.call-start = ((), (), s32[]{:S(2)}) async-start(), calls=%async_computation.11 | async-start | bytes 1843200 | tf_op jit(solution)/shard_map/reduce_scatter | solution.py:268
  572.7 7.7 copy-start.50
  572.7 7.7 copy-start.56
  580.4 17.7 %copy-start.23 = (bf16[1152,256]{1,0:T(8,128)(2,1)S(1)}, bf16[1152,256]{1,0:T(8,128)(2,1)}, u32[]{:S(2)}) copy-start(bf16[1152,256]{1,0:T(8,128)(2,1)} %copy-done.22) | copy-start | bytes 1769476
  585.8 14.2 %copy-start.27 = (bf16[640,256]{1,0:T(8,128)(2,1)S(1)}, bf16[640,256]{1,0:T(8,128)(2,1)}, u32[]{:S(2)}) copy-start(bf16[640,256]{1,0:T(8,128)(2,1)} %copy-done.26) | copy-start | bytes 983044
  610.4 7.6 copy-start.10
  721.7 36.6 %collective-permute-start.2 = (bf16[40,256]{1,0:T(8,128)(2,1)S(1)}, bf16[40,256]{1,0:T(8,128)(2,1)S(1)}, u32[]{:S(2)}, u32[]{:S(2)}) collective-permute-start(bf16[40,256]{1,0:T(8,128)(2,1)S(1)} %get-tuple-element.54), channel_id=1, source_target_pairs={{0,12},{4,16},{8,20},{12,24},{16,28},{20,32},{24,36},{28,40},{32,4... | collective-permute-start | bytes 61448
  723.0 26.1 %collective-permute-start.19 = (bf16[4,1728]{1,0:T(4,128)(2,1)S(1)}, bf16[4,1728]{1,0:T(4,128)(2,1)S(1)}, u32[]{:S(2)}, u32[]{:S(2)}) collective-permute-start(bf16[4,1728]{1,0:T(4,128)(2,1)S(1)} %slice.44), channel_id=1, source_target_pairs={{0,16},{4,20},{8,24},{12,28},{16,32},{20,36},{24,40},{28,44},{32,4... | collective-permute-start | bytes 41480
  724.3 30.0 %collective-permute-start.23 = (bf16[4,1728]{1,0:T(4,128)(2,1)S(1)}, bf16[4,1728]{1,0:T(4,128)(2,1)}, u32[]{:S(2)}, u32[]{:S(2)}) collective-permute-start(bf16[4,1728]{1,0:T(4,128)(2,1)S(1)} %slice.45), channel_id=1, source_target_pairs={{0,16},{4,20},{8,24},{12,28},{16,32},{20,36},{24,40},{28,44},{32,4... | collective-permute-start | bytes 41480
  730.0 7.5 collective-permute-start.3
  732.1 8.3 collective-permute-start.7
  737.5 8.3 collective-permute-start.11
  740.5 6.5 collective-permute-start.15
  745.7 14.1 %collective-permute-start.1 = (bf16[40,256]{1,0:T(8,128)(2,1)S(1)}, bf16[40,256]{1,0:T(8,128)(2,1)S(1)}, u32[]{:S(2)}, u32[]{:S(2)}) collective-permute-start(bf16[40,256]{1,0:T(8,128)(2,1)S(1)} %get-tuple-element.54), channel_id=1, source_target_pairs={{0,8},{4,12},{8,16},{12,20},{16,24},{20,28},{24,32},{28,36},{32,40... | collective-permute-start | bytes 61448
  747.0 16.1 %collective-permute-start = (bf16[40,256]{1,0:T(8,128)(2,1)S(1)}, bf16[40,256]{1,0:T(8,128)(2,1)S(1)}, u32[]{:S(2)}, u32[]{:S(2)}) collective-permute-start(bf16[40,256]{1,0:T(8,128)(2,1)S(1)} %get-tuple-element.54), channel_id=1, source_target_pairs={{0,4},{4,8},{8,12},{12,16},{16,20},{20,24},{24,28},{28,32},{32,36}... | collective-permute-start | bytes 61448
  749.1 17.7 %collective-permute-start.6 = (bf16[40,256]{1,0:T(8,128)(2,1)S(1)}, bf16[40,256]{1,0:T(8,128)(2,1)S(1)}, u32[]{:S(2)}, u32[]{:S(2)}) collective-permute-start(bf16[40,256]{1,0:T(8,128)(2,1)S(1)} %get-tuple-element.55), channel_id=1, source_target_pairs={{0,12},{4,16},{8,20},{12,24},{16,28},{20,32},{24,36},{28,40},{32,4... | collective-permute-start | bytes 61448
  754.3 15.1 %collective-permute-start.5 = (bf16[40,256]{1,0:T(8,128)(2,1)S(1)}, bf16[40,256]{1,0:T(8,128)(2,1)S(1)}, u32[]{:S(2)}, u32[]{:S(2)}) collective-permute-start(bf16[40,256]{1,0:T(8,128)(2,1)S(1)} %get-tuple-element.55), channel_id=1, source_target_pairs={{0,8},{4,12},{8,16},{12,20},{16,24},{20,28},{24,32},{28,36},{32,40... | collective-permute-start | bytes 61448
  758.3 14.8 %collective-permute-start.4 = (bf16[40,256]{1,0:T(8,128)(2,1)S(1)}, bf16[40,256]{1,0:T(8,128)(2,1)S(1)}, u32[]{:S(2)}, u32[]{:S(2)}) collective-permute-start(bf16[40,256]{1,0:T(8,128)(2,1)S(1)} %get-tuple-element.55), channel_id=1, source_target_pairs={{0,4},{4,8},{8,12},{12,16},{16,20},{20,24},{24,28},{28,32},{32,36}... | collective-permute-start | bytes 61448
  759.8 18.7 %collective-permute-start.10 = (bf16[40,256]{1,0:T(8,128)(2,1)S(1)}, bf16[40,256]{1,0:T(8,128)(2,1)S(1)}, u32[]{:S(2)}, u32[]{:S(2)}) collective-permute-start(bf16[40,256]{1,0:T(8,128)(2,1)S(1)} %get-tuple-element.56), channel_id=1, source_target_pairs={{0,12},{4,16},{8,20},{12,24},{16,28},{20,32},{24,36},{28,40},{32,4... | collective-permute-start | bytes 61448
  763.1 17.8 %collective-permute-start.9 = (bf16[40,256]{1,0:T(8,128)(2,1)S(1)}, bf16[40,256]{1,0:T(8,128)(2,1)S(1)}, u32[]{:S(2)}, u32[]{:S(2)}) collective-permute-start(bf16[40,256]{1,0:T(8,128)(2,1)S(1)} %get-tuple-element.56), channel_id=1, source_target_pairs={{0,8},{4,12},{8,16},{12,20},{16,24},{20,28},{24,32},{28,36},{32,40... | collective-permute-start | bytes 61448
  766.8 16.0 %collective-permute-start.14 = (bf16[40,256]{1,0:T(8,128)(2,1)S(1)}, bf16[40,256]{1,0:T(8,128)(2,1)S(1)}, u32[]{:S(2)}, u32[]{:S(2)}) collective-permute-start(bf16[40,256]{1,0:T(8,128)(2,1)S(1)} %get-tuple-element.57), channel_id=1, source_target_pairs={{0,12},{4,16},{8,20},{12,24},{16,28},{20,32},{24,36},{28,40},{32,4... | collective-permute-start | bytes 61448
  769.4 16.0 %collective-permute-start.13 = (bf16[40,256]{1,0:T(8,128)(2,1)S(1)}, bf16[40,256]{1,0:T(8,128)(2,1)S(1)}, u32[]{:S(2)}, u32[]{:S(2)}) collective-permute-start(bf16[40,256]{1,0:T(8,128)(2,1)S(1)} %get-tuple-element.57), channel_id=1, source_target_pairs={{0,8},{4,12},{8,16},{12,20},{16,24},{20,28},{24,32},{28,36},{32,40... | collective-permute-start | bytes 61448
  773.1 14.1 %collective-permute-start.12 = (bf16[40,256]{1,0:T(8,128)(2,1)S(1)}, bf16[40,256]{1,0:T(8,128)(2,1)S(1)}, u32[]{:S(2)}, u32[]{:S(2)}) collective-permute-start(bf16[40,256]{1,0:T(8,128)(2,1)S(1)} %get-tuple-element.57), channel_id=1, source_target_pairs={{0,4},{4,8},{8,12},{12,16},{16,20},{20,24},{24,28},{28,32},{32,36}... | collective-permute-start | bytes 61448
  778.4 12.2 %collective-permute-start.8 = (bf16[40,256]{1,0:T(8,128)(2,1)S(1)}, bf16[40,256]{1,0:T(8,128)(2,1)S(1)}, u32[]{:S(2)}, u32[]{:S(2)}) collective-permute-start(bf16[40,256]{1,0:T(8,128)(2,1)S(1)} %get-tuple-element.56), channel_id=1, source_target_pairs={{0,4},{4,8},{8,12},{12,16},{16,20},{20,24},{24,28},{28,32},{32,36}... | collective-permute-start | bytes 61448
  781.0 13.0 %collective-permute-start.18 = (bf16[40,1728]{1,0:T(8,128)(2,1)S(1)}, bf16[40,1728]{1,0:T(8,128)(2,1)S(1)}, u32[]{:S(2)}, u32[]{:S(2)}) collective-permute-start(bf16[40,1728]{1,0:T(8,128)(2,1)S(1)} %get-tuple-element.58), channel_id=1, source_target_pairs={{0,12},{4,16},{8,20},{12,24},{16,28},{20,32},{24,36},{28,40},{32,4... | collective-permute-start | bytes 414728
  782.9 13.6 %collective-permute-start.17 = (bf16[40,1728]{1,0:T(8,128)(2,1)S(1)}, bf16[40,1728]{1,0:T(8,128)(2,1)S(1)}, u32[]{:S(2)}, u32[]{:S(2)}) collective-permute-start(bf16[40,1728]{1,0:T(8,128)(2,1)S(1)} %get-tuple-element.58), channel_id=1, source_target_pairs={{0,8},{4,12},{8,16},{12,20},{16,24},{20,28},{24,32},{28,36},{32,40... | collective-permute-start | bytes 414728
  785.4 12.6 %collective-permute-start.16 = (bf16[40,1728]{1,0:T(8,128)(2,1)S(1)}, bf16[40,1728]{1,0:T(8,128)(2,1)S(1)}, u32[]{:S(2)}, u32[]{:S(2)}) collective-permute-start(bf16[40,1728]{1,0:T(8,128)(2,1)S(1)} %get-tuple-element.58), channel_id=1, source_target_pairs={{0,4},{4,8},{8,12},{12,16},{16,20},{20,24},{24,28},{28,32},{32,36}... | collective-permute-start | bytes 414728
  787.1 13.7 %collective-permute-start.22 = (bf16[40,1728]{1,0:T(8,128)(2,1)S(1)}, bf16[40,1728]{1,0:T(8,128)(2,1)S(1)}, u32[]{:S(2)}, u32[]{:S(2)}) collective-permute-start(bf16[40,1728]{1,0:T(8,128)(2,1)S(1)} %get-tuple-element.59), channel_id=1, source_target_pairs={{0,12},{4,16},{8,20},{12,24},{16,28},{20,32},{24,36},{28,40},{32,4... | collective-permute-start | bytes 414728
  790.7 13.4 %collective-permute-start.21 = (bf16[40,1728]{1,0:T(8,128)(2,1)S(1)}, bf16[40,1728]{1,0:T(8,128)(2,1)S(1)}, u32[]{:S(2)}, u32[]{:S(2)}) collective-permute-start(bf16[40,1728]{1,0:T(8,128)(2,1)S(1)} %get-tuple-element.59), channel_id=1, source_target_pairs={{0,8},{4,12},{8,16},{12,20},{16,24},{20,28},{24,32},{28,36},{32,40... | collective-permute-start | bytes 414728
  794.0 12.4 %collective-permute-start.20 = (bf16[40,1728]{1,0:T(8,128)(2,1)S(1)}, bf16[40,1728]{1,0:T(8,128)(2,1)}, u32[]{:S(2)}, u32[]{:S(2)}) collective-permute-start(bf16[40,1728]{1,0:T(8,128)(2,1)S(1)} %get-tuple-element.59), channel_id=1, source_target_pairs={{0,4},{4,8},{8,12},{12,16},{16,20},{20,24},{24,28},{28,32},{32,36}... | collective-permute-start | bytes 414728
  796.5 12.3 %collective-permute-start.26 = (bf16[40,1728]{1,0:T(8,128)(2,1)S(1)}, bf16[40,1728]{1,0:T(8,128)(2,1)S(1)}, u32[]{:S(2)}, u32[]{:S(2)}) collective-permute-start(bf16[40,1728]{1,0:T(8,128)(2,1)S(1)} %get-tuple-element.60), channel_id=1, source_target_pairs={{0,12},{4,16},{8,20},{12,24},{16,28},{20,32},{24,36},{28,40},{32,4... | collective-permute-start | bytes 414728
  798.0 10.9 %collective-permute-start.25 = (bf16[40,1728]{1,0:T(8,128)(2,1)S(1)}, bf16[40,1728]{1,0:T(8,128)(2,1)}, u32[]{:S(2)}, u32[]{:S(2)}) collective-permute-start(bf16[40,1728]{1,0:T(8,128)(2,1)S(1)} %get-tuple-element.60), channel_id=1, source_target_pairs={{0,8},{4,12},{8,16},{12,20},{16,24},{20,28},{24,32},{28,36},{32,40... | collective-permute-start | bytes 414728
  800.9 8.6 collective-permute-start.24
  804.1 4.7 collective-permute-start.27
  806.3 10.0 %copy-start.46 = (bf16[256]{0:T(256)(128)(2,1)S(1)}, bf16[256]{0:T(256)(128)(2,1)}, u32[]{:S(2)}) copy-start(bf16[256]{0:T(256)(128)(2,1)} %get-tuple-element.21) | copy-start | bytes 1540
  806.3 155.0 %copy-start.7 = (f32[160,1152]{1,0:T(8,128)S(1)}, f32[160,1152]{1,0:T(8,128)}, u32[]{:S(2)}) copy-start(f32[160,1152]{1,0:T(8,128)} %copy-done.6) | copy-start | bytes 2211844
  (32 other events, 54.1 us)
Sparse Core Ops, SparseCore 0:
  147.6 23.1 all-gather.14
  253.2 36.2 reduce-scatter.18
  444.6 36.9 reduce-scatter.20
  485.7 25.4 all-gather.18
  530.3 36.9 reduce-scatter.22
  572.5 25.4 all-gather.20
  610.5 25.3 reduce-scatter.24
Sparse Core Ops, SparseCore 1:
  255.9 45.7 all-gather.22
  303.8 45.7 all-gather.24
  351.7 45.7 all-gather.26
  399.8 25.1 all-gather.16
where the time goes:
time: 980 us; the launch traced here: 972 us
  blocking collectives  461 us (47%)
  waiting for transfers between devices  258 us (26%)
  starting transfers between devices  78.2 us (8%)
  matrix products  76 us (8%)
  local copies, waits for them, and re-layouts  45.5 us (5%)
  other arithmetic  32 us (3%)
  between operations  21 us (2%)
    unnamed x3, blocking collectives  351 us
    unnamed x28, starting transfers between devices  76.9 us
    unnamed x156, local copies, waits for them, and re-layouts  45.5 us
    all_gather x1, waiting for transfers between devices, local(): lax.all_gather(w_down, 'dp', axis=1, tiled=True)  40.7 us
    all_gather x1, waiting for transfers between devices, local(): lax.all_gather(w_up, 'dp', axis=0, tiled=True)  40.7 us
    reduce_scatter x1, waiting for transfers between devices, local(): lax.psum_scatter(contract_cols(grad_gate_in, back_gate) + contract_cols(g...  37.1 us
    reduce_scatter x1, waiting for transfers between devices, local(): lax.psum_scatter(jnp.dot(act, full_down, preferred_element_type=jnp.float...  36.9 us
    reduce_scatter x1, waiting for transfers between devices, local(): lax.psum_scatter(jnp.dot(heads_out, full_out, preferred_element_type=jnp....  34.6 us
  transfers between devices with their start and end apart: 39, of which 9 were waited for; matrix products, arithmetic and copies ran while one was open for 17% of the time, Pallas kernels for 0%

commit v1 on v0

v1 whole, which is shorter than its diff:
```python
import functools
import math

import jax
import jax.numpy as jnp
from jax import lax
from jax.experimental import pallas as pl
from jax.experimental.pallas import tpu as pltpu
from jax.sharding import PartitionSpec as P

WINDOW = 512
EPSILON = 1e-06
ROPE_BASE = 10000.0
GELU_SCALE = math.sqrt(2.0 / math.pi)
MASKED = -1e30
BF16 = jnp.bfloat16
F32 = jnp.float32
ROWS = 160
WIDTH = 1152
CHUNK = 72
FFPAD = 1792
ATTN_COLS = 1280
MESH = pl.DeviceIdType.MESH


def normalize(inputs):
    inverse = lax.rsqrt(jnp.mean(inputs * inputs, axis=-1, keepdims=True) + EPSILON)
    return (inputs * inverse, inverse)


def normalize_back(grad_hat, normed, inverse):
    return inverse * (grad_hat - normed * jnp.mean(grad_hat * normed, axis=-1, keepdims=True))


def rotary_tables(places, width):
    half = width // 2
    freqs = ROPE_BASE ** (-(jnp.arange(half, dtype=jnp.float32) * 2.0) / width)
    angles = places.astype(jnp.float32)[:, None] * freqs[None, :]
    return (jnp.cos(angles), jnp.sin(angles))


def rotate(inputs, cosine, sine):
    half = inputs.shape[-1] // 2
    first = inputs[:, :half]
    second = inputs[:, half:]
    return jnp.concatenate(
        [first * cosine - second * sine, second * cosine + first * sine], axis=-1
    )


def gelu_parts(inputs):
    inner = GELU_SCALE * (inputs + 0.044715 * inputs * inputs * inputs)
    tangent = jnp.tanh(inner)
    result = 0.5 * inputs * (1.0 + tangent)
    slope = 0.5 * (1.0 + tangent) + 0.5 * inputs * (1.0 - tangent * tangent) * GELU_SCALE * (
        1.0 + 3.0 * 0.044715 * inputs * inputs
    )
    return (result, slope)


def window_mask(segments):
    length = segments.shape[0]
    places = jnp.arange(length, dtype=jnp.int32)
    offset = places[:, None] - places[None, :]
    same = segments[:, None] == segments[None, :]
    return same & (offset >= 0) & (offset < WINDOW)


def contract_rows(left, right):
    return lax.dot_general(
        left, right, (((0,), (0,)), ((), ())), preferred_element_type=jnp.float32
    )


def contract_cols(left, right):
    return lax.dot_general(
        left, right, (((1,), (1,)), ((), ())), preferred_element_type=jnp.float32
    )


def attend_scores(queries, keys, allowed, scale):
    return jnp.where(allowed, contract_cols(queries, keys) * scale, MASKED)


def attend_forward(queries, keys, values, allowed, scale):
    scores = attend_scores(queries, keys, allowed, scale)
    top = jnp.max(scores, axis=-1, keepdims=True)
    totals = jnp.sum(jnp.exp(scores - top), axis=-1, keepdims=True)
    logsum = top + jnp.log(totals)
    probs = jnp.exp(scores - logsum).astype(jnp.bfloat16)
    return (jnp.dot(probs, values, preferred_element_type=jnp.float32), logsum)


def attend_backward(queries, keys, values, allowed, scale, logsum, grad_heads):
    probs = jnp.exp(attend_scores(queries, keys, allowed, scale) - logsum)
    grad_values = contract_rows(probs.astype(jnp.bfloat16), grad_heads)
    grad_probs = contract_cols(grad_heads, values)
    centre = jnp.sum(probs * grad_probs, axis=-1, keepdims=True)
    grad_scores = (probs * (grad_probs - centre) * scale).astype(jnp.bfloat16)
    grad_queries = jnp.dot(grad_scores, keys, preferred_element_type=jnp.float32)
    grad_keys = contract_rows(grad_scores, queries)
    return (grad_queries, grad_keys, grad_values)


def wrap(value):
    return lax.rem(value + 8, 4)


class Place:
    def __init__(self):
        dp = lax.axis_index("dp")
        self.z = lax.axis_index("tensor")
        self.core = lax.rem(dp, 2)
        self.x = lax.rem(dp // 2, 4)
        self.y = dp // 8
        self.s = 1 - 2 * self.core

    def device(self, y=None, x=None, core=None, z=None):
        y = self.y if y is None else y
        x = self.x if x is None else x
        core = self.core if core is None else core
        z = self.z if z is None else z
        return ((y * 4 + x) * 2 + core, z)

    def partner(self):
        return self.device(core=1 - self.core)

    def greet(self, xy, far_z=False):
        barrier = pltpu.get_barrier_semaphore()
        others = [self.device(z=wrap(self.z + 1)), self.device(z=wrap(self.z - 1))]
        if xy:
            others += [
                self.partner(),
                self.device(x=wrap(self.x + 1)),
                self.device(x=wrap(self.x - 1)),
                self.device(y=wrap(self.y + 1)),
                self.device(y=wrap(self.y - 1)),
            ]
        if far_z:
            others.append(self.device(z=wrap(self.z + 2)))
        for other in others:
            pl.semaphore_signal(barrier, inc=1, device_id=other, device_id_type=MESH)
        pl.semaphore_wait(barrier, len(others))


def remote(src, dst, send, recv, device):
    return pltpu.make_async_remote_copy(
        src_ref=src,
        dst_ref=dst,
        send_sem=send,
        recv_sem=recv,
        device_id=device,
        device_id_type=MESH,
    )


def run_streams(streams):
    streams = list(streams)
    while streams:
        alive = []
        for stream in streams:
            try:
                next(stream)
                alive.append(stream)
            except StopIteration:
                pass
        streams = alive


def halves(n):
    tiles = n // 256
    a = (tiles + 1) // 2
    return (a * 128, (tiles - a) * 128)


class Axes:
    def __init__(self, place, which, n):
        wa, wb = halves(n)
        self.which = which
        self.w = wa if which == 0 else wb
        start = 0 if which == 0 else wa
        self.place = place
        self.mine = pl.ds(pl.multiple_of(place.core * (n // 2) + start, 128), self.w)
        self.theirs = pl.ds(pl.multiple_of((1 - place.core) * (n // 2) + start, 128), self.w)
        self.u, self.v = (place.x, place.y) if which == 0 else (place.y, place.x)

    def device(self, u=None, v=None):
        u = self.u if u is None else u
        v = self.v if v is None else v
        return self.place.device(y=v, x=u) if self.which == 0 else self.place.device(y=u, x=v)

    def chunk(self, ref, u, v, cols):
        return ref.at[v, u, :, cols] if self.which == 0 else ref.at[u, v, :, cols]

    def group(self, ref, v, cols):
        return ref.at[v, :, :, cols] if self.which == 0 else ref.at[:, v, :, cols]


def merge_own(place, own, other, both, send, recv):
    copy = remote(own, other, send, recv, place.partner())
    copy.start()
    yield
    copy.wait()
    mine = own[...].astype(F32)
    theirs = other[...].astype(F32)
    first = place.core == 0
    both[...] = jnp.concatenate(
        [jnp.where(first, mine, theirs), jnp.where(first, theirs, mine)], axis=0
    ).astype(BF16)


def gather_half(ax, both, out, ring_send, ring_recv, chip_send, chip_recv):
    place, s = ax.place, ax.place.s
    cols = ax.mine
    sent = []

    def send(src, u, v, device, k):
        copy = remote(src, ax.chunk(out, u, v, cols), ring_send.at[k], ring_recv.at[k], device)
        copy.start()
        sent.append(copy)

    def arrive(u, v, k):
        here = ax.chunk(out, u, v, cols)
        remote(here, here, ring_send.at[k], ring_recv.at[k], place.partner()).wait_recv()
        copy = remote(here, here, chip_send.at[k], chip_recv.at[k], place.partner())
        copy.start()
        sent.append(copy)

    def along_v(src, u, r):
        send(src, u, ax.v, ax.device(v=wrap(ax.v + s)), 3 + 3 * r)
        send(src, u, ax.v, ax.device(v=wrap(ax.v - s)), 4 + 3 * r)

    own = both.at[:, cols]
    us = [ax.u, wrap(ax.u - s), wrap(ax.u + s), wrap(ax.u + 2)]
    send(own, ax.u, ax.v, ax.device(u=wrap(ax.u + s)), 0)
    send(own, ax.u, ax.v, ax.device(u=wrap(ax.u - s)), 1)
    along_v(own, ax.u, 0)
    yield
    arrive(us[1], ax.v, 0)
    src = ax.chunk(out, us[1], ax.v, cols)
    send(src, us[1], ax.v, ax.device(u=wrap(ax.u + s)), 2)
    along_v(src, us[1], 1)
    yield
    arrive(us[2], ax.v, 1)
    along_v(ax.chunk(out, us[2], ax.v, cols), us[2], 2)
    yield
    for r in range(4):
        if r == 1:
            arrive(us[3], ax.v, 2)
            along_v(ax.chunk(out, us[3], ax.v, cols), us[3], 3)
            yield
        v = wrap(ax.v - s)
        arrive(us[r], v, 3 + 3 * r)
        send(ax.chunk(out, us[r], v, cols), us[r], v, ax.device(v=wrap(ax.v + s)), 5 + 3 * r)
        yield
        arrive(us[r], wrap(ax.v + s), 4 + 3 * r)
        yield
    for r in range(4):
        arrive(us[r], wrap(ax.v + 2), 5 + 3 * r)
        yield
    for copy in sent:
        copy.wait_send()
    yield
    theirs = [ax.u, wrap(ax.u + s), wrap(ax.u - s), wrap(ax.u + 2)]
    landing = [(theirs[1], ax.v), (theirs[2], ax.v), (theirs[3], ax.v)]
    for r in range(4):
        landing += [(theirs[r], wrap(ax.v + s)), (theirs[r], wrap(ax.v - s)), (theirs[r], wrap(ax.v + 2))]
    for k, (u, v) in enumerate(landing):
        here = ax.chunk(out, u, v, ax.theirs)
        remote(here, here, chip_send.at[k], chip_recv.at[k], place.partner()).wait_recv()


def gather_stream(place, own, out, scratch):
    other, both, sems, local = scratch
    n = own.shape[1]
    yield from merge_own(place, own, other, both, sems.at[0, 0, 0, 15], sems.at[0, 0, 1, 15])
    keep = pltpu.make_async_copy(both, out.at[place.y, place.x], local)
    keep.start()
    parts = [
        gather_half(
            Axes(place, h, n), both, out, sems.at[h, 0, 0], sems.at[h, 0, 1], sems.at[h, 1, 0], sems.at[h, 1, 1]
        )
        for h in (0, 1)
    ]
    while parts:
        alive = []
        for part in parts:
            try:
                next(part)
                alive.append(part)
            except StopIteration:
                pass
        parts = alive
        yield
    keep.wait()


def gather_scratch(n):
    return [
        pltpu.VMEM((36, n), BF16),
        pltpu.VMEM((CHUNK, n), BF16),
        pltpu.SemaphoreType.DMA((2, 2, 2, 16)),
        pltpu.SemaphoreType.DMA,
    ]


def add_chunks(count, target, *terms):
    def body(i, carry):
        total = terms[0](i)[...].astype(F32)
        for term in terms[1:]:
            total = total + term(i)[...].astype(F32)
        target(i)[...] = total.astype(BF16)
        return carry

    if count == 1:
        body(0, 0)
    else:
        lax.fori_loop(0, count, body, 0)


def scatter_half(ax, grads, final, bufs, sems):
    held, got, b1, b2, b3, c1, c2, c3, total = bufs
    place, s = ax.place, ax.place.s
    vs = [wrap(ax.v + 2), wrap(ax.v - s), wrap(ax.v + s), ax.v]
    for_partner = [wrap(ax.v + 2), wrap(ax.v + s), wrap(ax.v - s), ax.v]
    sent, loads, gets = [], [], []
    for k in range(4):
        give = remote(
            ax.group(grads, for_partner[k], ax.theirs),
            got.at[k],
            sems.at[0, k],
            sems.at[1, k],
            place.partner(),
        )
        give.start()
        sent.append(give)
        gets.append(give)
        load = pltpu.make_async_copy(ax.group(grads, vs[k], ax.mine), held.at[k], sems.at[2, k])
        load.start()
        loads.append(load)
    yield

    def chip_sum(k):
        loads[k].wait()
        gets[k].wait_recv()
        add_chunks(4, lambda i: got.at[k, i], lambda i: got.at[k, i], lambda i: held.at[k, i])

    def send(src, dst, k, device):
        copy = remote(src, dst, sems.at[0, k], sems.at[1, k], device)
        copy.start()
        sent.append(copy)
        return copy

    chip_sum(0)
    far = send(got.at[0], b1, 4, ax.device(v=wrap(ax.v + s)))
    yield
    chip_sum(1)
    back = send(got.at[1], b2, 5, ax.device(v=wrap(ax.v - s)))
    yield
    chip_sum(2)
    yield
    far.wait_recv()
    add_chunks(4, lambda i: b1.at[i], lambda i: b1.at[i], lambda i: got.at[2, i])
    forth = send(b1, b3, 6, ax.device(v=wrap(ax.v + s)))
    yield
    loads[3].wait()
    gets[3].wait_recv()
    back.wait_recv()
    yield
    forth.wait_recv()
    add_chunks(
        4,
        lambda i: total.at[i],
        lambda i: got.at[3, i],
        lambda i: held.at[3, i],
        lambda i: b2.at[i],
        lambda i: b3.at[i],
    )
    far = send(total.at[wrap(ax.u + 2)], c1, 7, ax.device(u=wrap(ax.u + s)))
    back = send(total.at[wrap(ax.u - s)], c2, 8, ax.device(u=wrap(ax.u - s)))
    yield
    far.wait_recv()
    add_chunks(1, lambda i: c1, lambda i: c1, lambda i: total.at[wrap(ax.u + s)])
    forth = send(c1, c3, 9, ax.device(u=wrap(ax.u + s)))
    yield
    back.wait_recv()
    forth.wait_recv()
    add_chunks(1, lambda i: c2, lambda i: total.at[ax.u], lambda i: c2, lambda i: c3)
    keep = pltpu.make_async_copy(c2, final.at[:, ax.mine], sems.at[2, 4])
    keep.start()
    last = send(c2, final.at[:, ax.mine], 10, place.partner())
    yield
    for copy in sent:
        copy.wait_send()
    keep.wait()
    remote(c2, final.at[:, ax.theirs], sems.at[0, 10], sems.at[1, 10], place.partner()).wait_recv()


def scatter_scratch(n):
    shapes = []
    for w in halves(n):
        shapes += [pltpu.VMEM((4, 4, CHUNK, w), BF16)] * 2
        shapes += [pltpu.VMEM((4, CHUNK, w), BF16)] * 3
        shapes += [pltpu.VMEM((CHUNK, w), BF16)] * 3
        shapes += [pltpu.VMEM((4, CHUNK, w), BF16)]
        shapes += [pltpu.SemaphoreType.DMA((3, 11))]
    return shapes


def scatter_streams(place, grads, final, scratch):
    n = grads.shape[3]
    for h in (0, 1):
        part = scratch[10 * h : 10 * h + 10]
        yield scatter_half(Axes(place, h, n), grads, final, part[:9], part[9])


def rows_gather(place, out, sems):
    s, z = place.s, place.z
    ahead, behind = place.device(z=wrap(z + s)), place.device(z=wrap(z - s))

    def copy(slot, k, device):
        return remote(out.at[slot], out.at[slot], sems.at[0, k], sems.at[1, k], device)

    first = copy(z, 0, ahead)
    first.start()
    second = copy(z, 1, behind)
    second.start()
    yield
    copy(wrap(z - s), 0, ahead).wait_recv()
    relay = copy(wrap(z - s), 2, ahead)
    relay.start()
    yield
    copy(wrap(z + s), 1, ahead).wait_recv()
    yield
    yield
    copy(wrap(z + 2), 2, ahead).wait_recv()
    for sent in (first, second, relay):
        sent.wait_send()


def rows_scatter(place, parts, bufs, sems):
    s, z = place.s, place.z
    b1, b2, b3 = bufs
    ahead, behind = place.device(z=wrap(z + s)), place.device(z=wrap(z - s))

    def copy(src, dst, k, device):
        return remote(src, dst, sems.at[0, k], sems.at[1, k], device)

    far = copy(parts.at[wrap(z + 2)], b1, 0, ahead)
    far.start()
    back = copy(parts.at[wrap(z - s)], b2, 1, behind)
    back.start()
    yield
    yield
    far.wait_recv()
    mid = wrap(z + s)

    def body(i, carry):
        rows = pl.ds(pl.multiple_of(i * 32, 32), 32)
        b1[rows, :] = (b1[rows, :].astype(F32) + parts[mid, rows, :].astype(F32)).astype(BF16)
        return carry

    lax.fori_loop(0, ROWS // 32, body, 0)
    forth = copy(b1, b3, 2, ahead)
    forth.start()
    yield
    back.wait_recv()
    yield
    forth.wait_recv()
    for sent in (far, back, forth):
        sent.wait_send()


def rows_scratch():
    return [pltpu.VMEM((ROWS, WIDTH), BF16)] * 3 + [pltpu.SemaphoreType.DMA((2, 3))] * 2


def row_blocks(body):
    def step(i, carry):
        body(pl.ds(pl.multiple_of(i * 16, 16), 16))
        return carry

    lax.fori_loop(0, ROWS // 16, step, 0)


def col_sum(ref, row, values):
    ref[8 * row : 8 * row + 8, :] = ref[8 * row : 8 * row + 8, :] + values[:8] + values[8:]


def start_kernel(tokens, attn_own, rows_out, mats_out, sems, *scratch):
    place = Place()
    place.greet(True)

    def z_stream():
        rows_out[place.z] = tokens[...]
        yield from rows_gather(place, rows_out, sems)

    run_streams([gather_stream(place, attn_own, mats_out, scratch), z_stream()])


def middle_kernel(parts, tokens, gains, own_g, own_u, own_d, rows_out, attn_sum, full_g, full_u, full_d, *scratch):
    place = Place()
    place.greet(True)
    b1, b2, b3, sems, sems2 = scratch[:5]

    def z_stream():
        yield from rows_scatter(place, parts, (b1, b2, b3), sems)

        def body(rows):
            total = (
                parts[place.z, rows, :].astype(F32) + b2[rows, :].astype(F32) + b3[rows, :].astype(F32)
            )
            attn_sum[rows, :] = total
            hat, _ = normalize(total)
            hidden = tokens[rows, :].astype(F32) + hat * gains[1:2, :]
            mid, _ = normalize(hidden)
            rows_out[place.z, rows, :] = (mid * gains[2:3, :]).astype(BF16)

        row_blocks(body)
        yield from rows_gather(place, rows_out, sems2)

    run_streams(
        [
            z_stream(),
            gather_stream(place, own_g, full_g, scratch[5:9]),
            gather_stream(place, own_u, full_u, scratch[9:13]),
            gather_stream(place, own_d, full_d, scratch[13:17]),
        ]
    )


def turn_kernel(parts, tokens, attn_sum, gains, cotangent, rows_out, layer_out, sums, *scratch):
    place = Place()
    place.greet(False)
    b1, b2, b3, sems, sems2 = scratch[:5]
    sums[...] = jnp.zeros_like(sums)

    def z_stream():
        yield from rows_scatter(place, parts, (b1, b2, b3), sems)

        def body(rows):
            total = (
                parts[place.z, rows, :].astype(F32) + b2[rows, :].astype(F32) + b3[rows, :].astype(F32)
            )
            attn_hat, _ = normalize(attn_sum[rows, :])
            hidden = tokens[rows, :].astype(F32) + attn_hat * gains[1:2, :]
            hat, inverse = normalize(total)
            layer_out[rows, :] = (hidden + hat * gains[3:4, :]).astype(BF16)
            grad = cotangent[rows, :].astype(F32)
            col_sum(sums, 0, grad * hat)
            rows_out[place.z, rows, :] = normalize_back(grad * gains[3:4, :], hat, inverse).astype(BF16)

        row_blocks(body)
        yield from rows_gather(place, rows_out, sems2)

    run_streams([z_stream()])


def back_kernel(
    parts, tokens, attn_sum, gains, cotangent, grad_g, grad_u, grad_d,
    rows_out, grad_hidden, sums, sum_g, sum_u, sum_d, *scratch
):
    place = Place()
    place.greet(True)
    b1, b2, b3, sems, sems2 = scratch[:5]
    sums[...] = jnp.zeros_like(sums)

    def z_stream():
        yield from rows_scatter(place, parts, (b1, b2, b3), sems)

        def body(rows):
            grad_mid = (
                parts[place.z, rows, :].astype(F32) + b2[rows, :].astype(F32) + b3[rows, :].astype(F32)
            )
            attn_hat, attn_inverse = normalize(attn_sum[rows, :])
            hidden = tokens[rows, :].astype(F32) + attn_hat * gains[1:2, :]
            mid, inverse = normalize(hidden)
            col_sum(sums, 0, grad_mid * mid)
            grad = cotangent[rows, :].astype(F32) + normalize_back(grad_mid * gains[2:3, :], mid, inverse)
            grad_hidden[rows, :] = grad
            col_sum(sums, 1, grad * attn_hat)
            rows_out[place.z, rows, :] = normalize_back(
                grad * gains[1:2, :], attn_hat, attn_inverse
            ).astype(BF16)

        row_blocks(body)
        yield from rows_gather(place, rows_out, sems2)

    streams = [z_stream()]
    for i, (grads, final) in enumerate(((grad_d, sum_d), (grad_g, sum_g), (grad_u, sum_u))):
        streams += list(scatter_streams(place, grads, final, scratch[5 + 20 * i : 25 + 20 * i]))
    run_streams(streams)


def end_kernel(parts, grads, grad_rows, final, shared, *scratch):
    place = Place()
    place.greet(True, far_z=True)
    b1, b2, b3, sems, sems2 = scratch[:5]
    got, zsend, zrecv = scratch[5:8]

    def z_stream():
        yield from rows_scatter(place, parts, (b1, b2, b3), sems)

        def body(rows):
            grad_rows[rows, :] = (
                parts[place.z, rows, :].astype(F32) + b2[rows, :].astype(F32) + b3[rows, :].astype(F32)
            )

        row_blocks(body)

    run_streams([z_stream()] + list(scatter_streams(place, grads, final, scratch[8:28])))
    cols = pl.ds(512, 768)
    copies = []
    for k in range(3):
        copy = remote(
            final.at[:, cols], got.at[k], zsend.at[k], zrecv.at[k], place.device(z=wrap(place.z + k + 1))
        )
        copy.start()
        copies.append(copy)
    for copy in copies:
        copy.wait()
    total = final[:, cols].astype(F32)
    for k in range(3):
        total = total + got[k].astype(F32)
    shared[...] = total


def call(kernel, outs, ins, spaces, out_spaces, scratch, ident):
    return pl.pallas_call(
        kernel,
        out_shape=[jax.ShapeDtypeStruct(shape, dtype) for shape, dtype in outs],
        in_specs=[pl.BlockSpec(memory_space=space) for space in spaces],
        out_specs=[pl.BlockSpec(memory_space=space) for space in out_spaces],
        scratch_shapes=scratch,
        compiler_params=pltpu.CompilerParams(
            collective_id=ident, has_side_effects=True, vmem_limit_bytes=60 * 1024 * 1024
        ),
        name=kernel.__name__,
    )(*ins)


def local(
    tokens,
    cotangent,
    segment_ids,
    positions,
    w_query,
    w_key,
    w_value,
    w_out,
    w_gate,
    w_up,
    w_down,
    prenorm_attn,
    postnorm_attn,
    prenorm_ffw,
    postnorm_ffw,
    query_norm,
    key_norm,
):
    vm, hbm = pltpu.VMEM, pl.ANY
    shard = 36
    core = lax.rem(lax.axis_index("dp"), 2)
    hidden_units = w_gate.shape[1]
    pad = ((0, 0), (0, FFPAD - hidden_units))
    width = w_key.shape[1]

    def column(vector):
        return jnp.pad(vector, (0, shard - vector.shape[0]))[:, None]

    attn_own = jnp.concatenate(
        [w_query, w_out.T, w_key, w_value]
        + [column(g) for g in (prenorm_attn, postnorm_attn, prenorm_ffw, postnorm_ffw, query_norm, key_norm)]
        + [jnp.zeros((shard, ATTN_COLS - 1024 - 6), BF16)],
        axis=1,
    )
    tokens_all, mats = call(
        start_kernel,
        [((4, ROWS, WIDTH), BF16), ((4, 4, CHUNK, ATTN_COLS), BF16)],
        [tokens, attn_own],
        [vm, vm],
        [vm, hbm],
        [pltpu.SemaphoreType.DMA((2, 3))] + gather_scratch(ATTN_COLS),
        0,
    )
    mats = mats.reshape(WIDTH, ATTN_COLS)
    full_query, full_out = mats[:, :256], mats[:, 256:512]
    full_key, full_value = mats[:, 512:768], mats[:, 768:1024]
    small = mats[:, 1024:1032].astype(F32).T
    gains = small
    gain_in = small[0]
    gain_query = small[4].reshape(32, shard)[:, :8].reshape(-1)
    gain_key = small[5].reshape(32, shard)[:, :8].reshape(-1)
    normed_all, _ = normalize(tokens_all.reshape(4 * ROWS, WIDTH).astype(F32))
    attn_rows = (normed_all * gain_in).astype(BF16)
    scale = 1.0 / math.sqrt(width)
    cosine, sine = rotary_tables(positions.reshape(-1), width)
    mask = window_mask(segment_ids[0])
    key_hat, key_inverse = normalize(jnp.dot(attn_rows, full_key, preferred_element_type=F32))
    keys = rotate(key_hat * gain_key, cosine, sine).astype(BF16)
    values = jnp.dot(attn_rows, full_value, preferred_element_type=F32).astype(BF16)
    query_hat, query_inverse = normalize(jnp.dot(attn_rows, full_query, preferred_element_type=F32))
    queries = rotate(query_hat * gain_query, cosine, sine).astype(BF16)
    piece, logsum = attend_forward(queries, keys, values, mask, scale)
    heads_out = piece.astype(BF16)
    attn_part = contract_cols(heads_out, full_out).astype(BF16)
    whole = ((4, 4, CHUNK, FFPAD), BF16)
    ffw_rows, attn_sum, full_gate, full_up, full_down = call(
        middle_kernel,
        [((4, ROWS, WIDTH), BF16), ((ROWS, WIDTH), F32), whole, whole, whole],
        [
            attn_part.reshape(4, ROWS, WIDTH),
            tokens,
            gains,
            jnp.pad(w_gate, pad),
            jnp.pad(w_up, pad),
            jnp.pad(w_down.T, pad),
        ],
        [vm] * 6,
        [vm, vm, hbm, hbm, hbm],
        rows_scratch() + gather_scratch(FFPAD) * 3,
        1,
    )
    ffw_rows = ffw_rows.reshape(4 * ROWS, WIDTH)
    full_gate = full_gate.reshape(WIDTH, FFPAD)
    full_up = full_up.reshape(WIDTH, FFPAD)
    full_down = full_down.reshape(WIDTH, FFPAD)
    gate = jnp.dot(ffw_rows, full_gate, preferred_element_type=F32)
    upward = jnp.dot(ffw_rows, full_up, preferred_element_type=F32)
    gelu_value, gelu_slope = gelu_parts(gate)
    act = (gelu_value * upward).astype(BF16)
    ffw_part = contract_cols(act, full_down).astype(BF16)
    grad_ffw, layer_out, ffw_sums = call(
        turn_kernel,
        [((4, ROWS, WIDTH), BF16), ((ROWS, WIDTH), BF16), ((8, WIDTH), F32)],
        [ffw_part.reshape(4, ROWS, WIDTH), tokens, attn_sum, gains, cotangent],
        [vm] * 5,
        [vm] * 3,
        rows_scratch(),
        2,
    )
    grad_ffw = grad_ffw.reshape(4 * ROWS, WIDTH)
    grad_down = contract_rows(grad_ffw, act).astype(BF16)
    grad_act = jnp.dot(grad_ffw, full_down, preferred_element_type=F32)
    grad_gate_in = (grad_act * upward * gelu_slope).astype(BF16)
    grad_up_in = (grad_act * gelu_value).astype(BF16)
    grad_gate = contract_rows(ffw_rows, grad_gate_in).astype(BF16)
    grad_up = contract_rows(ffw_rows, grad_up_in).astype(BF16)
    mid_part = (contract_cols(grad_gate_in, full_gate) + contract_cols(grad_up_in, full_up)).astype(BF16)
    split = (4, 4, CHUNK, FFPAD)
    final = ((CHUNK, FFPAD), BF16)
    grad_attn, grad_hidden, mid_sums, sum_gate, sum_up, sum_down = call(
        back_kernel,
        [((4, ROWS, WIDTH), BF16), ((ROWS, WIDTH), F32), ((16, WIDTH), F32), final, final, final],
        [
            mid_part.reshape(4, ROWS, WIDTH),
            tokens,
            attn_sum,
            gains,
            cotangent,
            grad_gate.reshape(split),
            grad_up.reshape(split),
            grad_down.reshape(split),
        ],
        [vm] * 5 + [hbm] * 3,
        [vm] * 6,
        rows_scratch() + scatter_scratch(FFPAD) * 3,
        3,
    )
    grad_attn = grad_attn.reshape(4 * ROWS, WIDTH)
    grad_output = contract_rows(grad_attn, heads_out)
    grad_heads = jnp.dot(grad_attn, full_out, preferred_element_type=F32).astype(BF16)
    grad_queries, grad_keys, grad_values = attend_backward(
        queries, keys, values, mask, scale, logsum, grad_heads
    )
    grad_query_turned = rotate(grad_queries, cosine, -sine)
    grad_query_norm = jnp.sum(grad_query_turned * query_hat, axis=0)
    query_in = normalize_back(grad_query_turned * gain_query, query_hat, query_inverse).astype(BF16)
    grad_key_turned = rotate(grad_keys, cosine, -sine)
    grad_key_norm = jnp.sum(grad_key_turned * key_hat, axis=0)
    key_in = normalize_back(grad_key_turned * gain_key, key_hat, key_inverse).astype(BF16)
    value_in = grad_values.astype(BF16)
    grad_query = contract_rows(attn_rows, query_in)
    grad_key = contract_rows(attn_rows, key_in)
    grad_value = contract_rows(attn_rows, value_in)
    in_part = contract_cols(query_in, full_query)
    in_part = in_part + contract_cols(key_in, full_key)
    in_part = in_part + contract_cols(value_in, full_value)
    grad_pre_attn = jnp.sum(in_part * normed_all, axis=0)

    def placed_rows(vector):
        return jnp.pad(vector.reshape(32, 8), ((0, 0), (0, shard - 8))).reshape(-1)

    vectors = jnp.stack(
        [
            grad_pre_attn,
            jnp.sum(mid_sums[8:], axis=0),
            jnp.sum(mid_sums[:8], axis=0),
            jnp.sum(ffw_sums, axis=0),
            placed_rows(grad_query_norm),
            placed_rows(grad_key_norm),
        ]
    )
    small_grads = jnp.pad(vectors, ((0, ATTN_COLS - 1024 - 6), (0, 0))).T
    grads = jnp.concatenate(
        [g.astype(BF16) for g in (grad_query, grad_output, grad_key, grad_value, small_grads)], axis=1
    )
    grad_in_rows, sum_attn, sum_shared = call(
        end_kernel,
        [((ROWS, WIDTH), F32), ((CHUNK, ATTN_COLS), BF16), ((CHUNK, ATTN_COLS - 512), F32)],
        [in_part.astype(BF16).reshape(4, ROWS, WIDTH), grads.reshape(4, 4, CHUNK, ATTN_COLS)],
        [vm, hbm],
        [vm] * 3,
        rows_scratch()
        + [
            pltpu.VMEM((3, CHUNK, ATTN_COLS - 512), BF16),
            pltpu.SemaphoreType.DMA((3,)),
            pltpu.SemaphoreType.DMA((3,)),
        ]
        + scatter_scratch(ATTN_COLS),
        4,
    )
    normed_in, inverse_in = normalize(tokens.astype(F32))
    grad_tokens = grad_hidden + normalize_back(grad_in_rows * gain_in, normed_in, inverse_in)

    def own_rows(array):
        first = core == 0
        return jnp.where(first, array[:shard], array[shard:]).astype(F32)

    own_attn = own_rows(sum_attn[:, :512])
    own_shared = own_rows(sum_shared)
    own_small = own_shared[:, 512:520]
    return (
        layer_out,
        grad_tokens,
        own_attn[:, :256],
        own_shared[:, :256],
        own_shared[:, 256:512],
        own_attn[:, 256:].T,
        own_rows(sum_gate)[:, :hidden_units],
        own_rows(sum_up)[:, :hidden_units],
        own_rows(sum_down)[:, :hidden_units].T,
        own_small[:, 0],
        own_small[:, 1],
        own_small[:, 2],
        own_small[:, 3],
        own_small[:8, 4],
        own_small[:8, 5],
    )


def solution(mesh):
    placed = (
        P(("dp", "tensor"), None),
        P(("dp", "tensor"), None),
        P("dp", None),
        P("dp", None),
        P("dp", "tensor"),
        P("dp", None),
        P("dp", None),
        P("tensor", "dp"),
        P("dp", "tensor"),
        P("dp", "tensor"),
        P("tensor", "dp"),
        P("dp"),
        P("dp"),
        P("dp"),
        P("dp"),
        P("dp"),
        P("dp"),
    )
    return jax.shard_map(
        local,
        mesh=mesh,
        in_specs=placed,
        out_specs=(
            P(("dp", "tensor"), None),
            P(("dp", "tensor"), None),
            P("dp", "tensor"),
            P("dp", None),
            P("dp", None),
            P("tensor", "dp"),
            P("dp", "tensor"),
            P("dp", "tensor"),
            P("tensor", "dp"),
            P("dp"),
            P("dp"),
            P("dp"),
            P("dp"),
            P("dp"),
            P("dp"),
        ),
        check_vma=False,
    )
```

time: 980 us -> 332 us (0.34)
  blocking collectives: 461 us -> 0 us
  waiting for transfers between devices: 258 us -> 0 us
  Pallas kernels: 0 us -> 219 us
  starting transfers between devices: 78.2 us -> 0 us
  local copies, waits for them, and re-layouts: 45.5 us -> 19.9 us
  between operations: 21 us -> 1.64 us
  other arithmetic: 32 us -> 15.6 us
    unnamed x3 -> x0, blocking collectives: 351 us -> none
    pallas_call x0 -> x5, Pallas kernels: none -> 219 us  [call(): pl.pallas_call(kernel, out_shape=[jax.ShapeDtypeStruct(shape, dtype) for...]
    all_gather x7 -> x0, waiting for transfers between devices: 147 us -> none  [the longest x1 40.7 us: local(): lax.all_gather(w_down, 'dp', axis=1, tiled=True)]
    reduce_scatter x4 -> x0, waiting for transfers between devices: 109 us -> none  [the longest x1 37.1 us: local(): lax.psum_scatter(contract_cols(grad_gate_in, back_gate) + contract_cols(g...]
    all_gather x4 -> x0, blocking collectives: 94.1 us -> none  [the longest x1 24.6 us: local(): lax.all_gather(w_out, 'dp', axis=1, tiled=True)]
    unnamed x28 -> x0, starting transfers between devices: 76.9 us -> none
    unnamed x156 -> x94, local copies, waits for them, and re-layouts: 45.5 us -> 3.23 us
    psum x1 -> x0, blocking collectives: 16.3 us -> none  [local(): lax.psum(rest[1].astype(jnp.bfloat16), 'tensor').astype(jnp.float32)]
  transfers between devices with their start and end apart: 39 -> 0, of which waited for: 9 -> 0; matrix products, arithmetic and copies ran while one was open for 17% -> 0% of each run, Pallas kernels for 0% -> 0%
where the time goes in v1:
time: 332 us; the launch traced here: 327 us
  Pallas kernels  219 us (66%)
  matrix products  70.9 us (21%)
  local copies, waits for them, and re-layouts  19.9 us (6%)
  other arithmetic  15.6 us (5%)
    pallas_call x5, Pallas kernels, call(): pl.pallas_call(kernel, out_shape=[jax.ShapeDtypeStruct(shape, dtype) for...  219 us
    dot_general x9, matrix products, contract_cols(): lax.dot_general(left, right, (((1,), (1,)), ((), ())), preferred_element_...  20 us
    dot_general x9, matrix products, contract_rows(): lax.dot_general(left, right, (((0,), (0,)), ((), ())), preferred_element_...  19.8 us
    dot_general x1, matrix products, local(): grad_act = jnp.dot(grad_ffw, full_down, preferred_element_type=F32)  10.4 us

profile of v1, /device:TPU:0, one launch (start us, length us, event | category | flops | bytes accessed | tf_op | source)
XLA Modules:
  0.0 326.9 jit_solution(526678789725202245)
XLA Ops:
  0.6 0.8 copy.40
  1.4 0.8 copy.41
  2.2 0.8 copy.42
  2.9 0.8 copy.43
  3.7 0.7 pad_bitcast_fusion.1
  4.5 0.7 pad_bitcast_fusion
  5.3 1.5 concatenate.20.attn_own
  6.8 35.1 %start_kernel.1 = (bf16[4,160,1152]{2,1,0:T(8,128)(2,1)}, bf16[4,4,72,1280]{3,2,1,0:T(8,128)(2,1)}) custom-call(bf16[160,1152]{1,0:T(8,128)(2,1)} %tokens.7, bf16[36,1280]{1,0:T(8,128)(2,1)} %concatenate.20.attn_own), custom_call_target="tpu_custom_call" | custom-call | tf_op jit(solution)/shard_map/start_kernel/pallas_call | solution.py:629
  41.9 1.1 slice.191
  43.1 0.6 copy-done.10
  43.8 1.7 multiply_reduce_fusion.1
  45.6 0.4 multiply_convert_fusion.2
  46.1 2.8 convolution_convert_fusion.12
  48.9 1.8 multiply_reduce_fusion.7
  51.2 2.2 multiply_reduce_fusion.8
  53.4 0.8 copy-done.2
  54.5 2.4 fusion.57
  56.9 1.6 fusion.77
  58.9 0.5 convolution_convert_fusion.11
  59.4 2.9 convolution_convert_fusion.3
  62.3 0.7 pad.33.own_g
  62.9 0.7 pad.34.own_u
  63.6 0.7 pad.35.own_d
  64.3 52.9 %middle_kernel.1 = (bf16[4,160,1152]{2,1,0:T(8,128)(2,1)}, f32[160,1152]{1,0:T(8,128)}, bf16[4,4,72,1792]{3,2,1,0:T(8,128)(2,1)}, bf16[4,4,72,1792]{3,2,1,0:T(8,128)(2,1)}, bf16[4,4,72,1792]{3,2,1,0:T(8,128)(2,1)}) custom-call(bf16[4,160,1152]{2,1,0:T(8,128)(2,1)} %bitcast.83, bf16[160,1152]{1,0:T(8,128)(2,1)} %tokens.7, f32[8,1152]{1,0:T(8,128)} %copy-done.10, ...), custom_call_target="tpu_custom_call" | custom-call | tf_op jit(solution)/shard_map/middle_kernel/pallas_call | solution.py:629
  117.2 5.9 %fusion.78 = f32[640,1792]{1,0:T(8,128)S(1)} fusion(bf16[640,1152]{1,0:T(8,128)(2,1)} %bitcast.114, bf16[1152,1792]{1,0:T(8,128)(2,1)} %bitcast.108), kind=kOutput, calls=%fused_computation.157 | convolution fusion | flops 2642411520 | bytes 10190848 | tf_op jit(solution)/shard_map/dot_general | solution.py:728
  123.2 4.8 %multiply_convert_fusion.1 = (bf16[640,1792]{1,0:T(8,128)(2,1)S(1)}, f32[640,1792]{1,0:T(8,128)}) fusion(f32[640,1792]{1,0:T(8,128)S(1)} %fusion.78, bf16[640,1152]{1,0:T(8,128)(2,1)S(1)} %bitcast.115, bf16[1152,1792]{1,0:T(8,128)(2,1)S(1)} %bitcast.106), kind=kOutput, calls=%fused_computation.13 | convolution fusion | flops 2653880320 | bytes 17072128 | tf_op jit(solution)/shard_map/dot_general | solution.py:729
  128.2 4.2 %convolution_convert_fusion.4 = bf16[640,1152]{1,0:T(8,128)(2,1)} fusion(bf16[640,1792]{1,0:T(8,128)(2,1)S(1)} %get-tuple-element.100, bf16[1152,1792]{1,0:T(8,128)(2,1)S(1)} %bitcast.111), kind=kOutput, calls=%fused_computation.20 | convolution fusion | flops 2643148800 | bytes 7897088 | tf_op jit(solution)/shard_map/dot_general | solution.py:76
  132.4 39.0 %turn_kernel.1 = (bf16[4,160,1152]{2,1,0:T(8,128)(2,1)}, bf16[160,1152]{1,0:T(8,128)(2,1)}, f32[8,1152]{1,0:T(8,128)}) custom-call(bf16[4,160,1152]{2,1,0:T(8,128)(2,1)} %bitcast.97, bf16[160,1152]{1,0:T(8,128)(2,1)} %tokens.7, f32[160,1152]{1,0:T(8,128)} %get-tuple-element.40.attn_sum, f32[8,1152]{1,0:T(8,128)} %copy-done.10, bf16[160,1152]{1,0:T(8,128)(2,1)} %cotangent.3), custom_call_target="tpu_custom_call" | custom-call | tf_op jit(solution)/shard_map/turn_kernel/pallas_call | solution.py:629
  171.4 10.4 %multiply_convert_fusion = (bf16[640,1792]{1,0:T(8,128)(2,1)S(1)}, bf16[640,1792]{1,0:T(8,128)(2,1)S(1)}) fusion(f32[640,1792]{1,0:T(8,128)} %copy-done.43, f32[640,1792]{1,0:T(8,128)} %get-tuple-element.101, bf16[640,1152]{1,0:T(8,128)(2,1)} %bitcast.118, bf16[1152,1792]{1,0:T(8,128)(2,1)} %bitcast.110), kind=kOutput, calls=%fused_computation.12 | convolution fusion | flops 2668789760 | bytes 19365888 | tf_op jit(solution)/shard_map/dot_general | solution.py:744
  181.9 3.2 fusion.79
  185.0 4.3 %fusion.7 = bf16[640,1152]{1,0:T(8,128)(2,1)} fusion(f32[640,1152]{1,0:T(8,128)S(1)} %fusion.79, bf16[640,1792]{1,0:T(8,128)(2,1)S(1)} %get-tuple-element.68, bf16[1152,1792]{1,0:T(8,128)(2,1)S(1)} %bitcast.107), kind=kOutput, calls=%fused_computation.19 | convolution fusion | flops 2643886080 | bytes 10846208 | tf_op jit(solution)/shard_map/dot_general | solution.py:76
  189.3 5.4 %convolution_convert_fusion.2 = bf16[1152,1792]{1,0:T(8,128)(2,1)} fusion(bf16[640,1152]{1,0:T(8,128)(2,1)S(1)} %bitcast.116, bf16[640,1792]{1,0:T(8,128)(2,1)S(1)} %get-tuple-element.69), kind=kOutput, calls=%fused_computation.2 | convolution fusion | flops 2644475904 | bytes 7897088 | tf_op jit(solution)/shard_map/dot_general | solution.py:70
  194.7 5.3 %convolution_convert_fusion.1 = bf16[1152,1792]{1,0:T(8,128)(2,1)} fusion(bf16[640,1152]{1,0:T(8,128)(2,1)S(1)} %bitcast.117, bf16[640,1792]{1,0:T(8,128)(2,1)S(1)} %get-tuple-element.68), kind=kOutput, calls=%fused_computation.1 | convolution fusion | flops 2644475904 | bytes 7897088 | tf_op jit(solution)/shard_map/dot_general | solution.py:70
  200.1 5.3 %convolution_convert_fusion = bf16[1152,1792]{1,0:T(8,128)(2,1)} fusion(bf16[640,1152]{1,0:T(8,128)(2,1)S(1)} %bitcast.119, bf16[640,1792]{1,0:T(8,128)(2,1)S(1)} %copy-done.45), kind=kOutput, calls=%fused_computation | convolution fusion | flops 2644475904 | bytes 7897088 | tf_op jit(solution)/shard_map/dot_general | solution.py:70
  205.4 48.9 %back_kernel.1 = (bf16[4,160,1152]{2,1,0:T(8,128)(2,1)}, f32[160,1152]{1,0:T(8,128)}, f32[16,1152]{1,0:T(8,128)}, bf16[72,1792]{1,0:T(8,128)(2,1)}, bf16[72,1792]{1,0:T(8,128)(2,1)}, /*index=5*/bf16[72,1792]{1,0:T(8,128)(2,1)}) custom-call(bf16[4,160,1152]{2,1,0:T(8,128)(2,1)} %bitcast.96, bf16[160,1152]{1,0:T(8,128)(2,1)} %tokens.7, ...), custom_call_target="tpu_custom_call" | custom-call | tf_op jit(solution)/shard_map/back_kernel/pallas_call | solution.py:629
  254.3 2.1 convolution_convert_fusion.10
  256.5 0.5 multiply_reduce_fusion.2
  257.4 0.5 copy-done.15
  258.0 0.5 fusion.67
  258.5 0.5 fusion.66
  258.9 1.5 fusion.54
  260.5 0.7 multiply_reduce_fusion.4
  261.3 0.6 fusion.31
  261.9 0.7 multiply_reduce_fusion.3
  262.8 0.7 convolution_add_fusion.1
  263.4 0.4 convolution_convert_fusion.9
  263.9 2.0 multiply_reduce_fusion
  265.9 0.7 fusion.10
  266.6 0.7 fusion.8
  267.3 0.7 fusion.11
  268.0 0.7 fusion.9
  269.5 3.5 %copy.47 = bf16[1152,1280]{1,0:T(8,128)(2,1)} copy(bf16[1152,1280]{0,1:T(8,128)(2,1)S(1)} %bitcast_dynamic-update-slice_fusion) | data formatting | bytes 5898240 | tf_op jit(solution)/shard_map/concatenate | solution.py:805
  273.0 43.0 %end_kernel.1 = (f32[160,1152]{1,0:T(8,128)}, bf16[72,1280]{1,0:T(8,128)(2,1)}, f32[72,768]{1,0:T(8,128)}) custom-call(bf16[4,160,1152]{2,1,0:T(8,128)(2,1)} %bitcast.82, bf16[4,4,72,1280]{3,2,1,0:T(8,128)(2,1)} %bitcast.81), custom_call_target="tpu_custom_call" | custom-call | tf_op jit(solution)/shard_map/end_kernel/pallas_call | solution.py:629
  316.2 1.4 fusion.19
  317.7 2.3 fusion.22
  320.0 0.9 select_convert_fusion
  320.9 0.6 slice_bitcast_fusion
  321.5 0.6 fusion.76
  322.2 0.7 fusion.69
  323.0 0.7 fusion.68
  323.8 0.7 convert_bitcast_fusion
  324.5 0.7 slice_reduce_fusion.2
  325.3 0.7 slice_reduce_fusion.9
  326.0 0.7 copy.54
  (135 shorter events, 3.5 us)
Async XLA Ops:
  41.9 3.8 %copy-start.1 = (bf16[4,160,1152]{2,1,0:T(8,128)(2,1)S(1)}, bf16[4,160,1152]{2,1,0:T(8,128)(2,1)}, u32[]{:S(2)}) copy-start(bf16[4,160,1152]{2,1,0:T(8,128)(2,1)} %get-tuple-element.34) | copy-start | bytes 4423684
  43.1 0.6 copy-start.10
  46.1 2.9 copy-start.5
  50.7 3.7 %copy-start.30 = (s32[1,640]{1,0:T(1,128)S(1)}, s32[1,640]{1,0:T(1,128)}, u32[]{:S(2)}) copy-start(s32[1,640]{1,0:T(1,128)} %param.20) | copy-start | bytes 7684
  51.1 5.7 %copy-start.27 = (f32[256]{0:T(256)}, f32[256]{0:T(256)S(1)}, u32[]{:S(2)}) copy-start(f32[256]{0:T(256)S(1)} %mul.306) | copy-start | bytes 3076
  53.4 0.8 copy-start.2
  53.4 3.4 %copy-start.29 = (s32[1,640]{1,0:T(1,128)S(1)}, s32[1,640]{1,0:T(1,128)}, u32[]{:S(2)}) copy-start(s32[1,640]{1,0:T(1,128)} %param.19) | copy-start | bytes 7684
  54.5 2.4 copy-start.33
  56.8 2.0 copy-start.11
  56.8 2.0 copy-start.13
  56.9 2.0 copy-start.7
  58.5 3.7 %copy-start.22 = (bf16[36,1728]{1,0:T(8,128)(2,1)S(1)}, bf16[36,1728]{1,0:T(8,128)(2,1)}, u32[]{:S(2)}) copy-start(bf16[36,1728]{1,0:T(8,128)(2,1)} %param.25) | copy-start | bytes 373252
  58.5 4.4 %copy-start.23 = (bf16[36,1728]{1,0:T(8,128)(2,1)S(1)}, bf16[36,1728]{1,0:T(8,128)(2,1)}, u32[]{:S(2)}) copy-start(bf16[36,1728]{1,0:T(8,128)(2,1)} %param.26) | copy-start | bytes 373252
  58.8 4.8 %copy-start.24 = (bf16[1728,36]{0,1:T(8,128)(2,1)S(1)}, bf16[1728,36]{0,1:T(8,128)(2,1)}, u32[]{:S(2)}) copy-start(bf16[1728,36]{0,1:T(8,128)(2,1)} %param.27) | copy-start | bytes 373252
  117.2 5.9 %copy-start.35 = (bf16[4,4,72,1792]{3,2,1,0:T(8,128)(2,1)S(1)}, bf16[4,4,72,1792]{3,2,1,0:T(8,128)(2,1)}, u32[]{:S(2)}) copy-start(bf16[4,4,72,1792]{3,2,1,0:T(8,128)(2,1)} %get-tuple-element.38) | copy-start | bytes 12386308
  117.2 5.9 %copy-start.40 = (bf16[4,160,1152]{2,1,0:T(8,128)(2,1)S(1)}, bf16[4,160,1152]{2,1,0:T(8,128)(2,1)}, u32[]{:S(2)}) copy-start(bf16[4,160,1152]{2,1,0:T(8,128)(2,1)} %get-tuple-element.36) | copy-start | bytes 4423684
  123.1 4.8 %copy-start.43 = (f32[640,1792]{1,0:T(8,128)}, f32[640,1792]{1,0:T(8,128)S(1)}, u32[]{:S(2)}) copy-start(f32[640,1792]{1,0:T(8,128)S(1)} %fusion.78) | copy-start | bytes 13762564
  123.2 5.0 %copy-start.38 = (bf16[4,4,72,1792]{3,2,1,0:T(8,128)(2,1)S(1)}, bf16[4,4,72,1792]{3,2,1,0:T(8,128)(2,1)}, u32[]{:S(2)}) copy-start(bf16[4,4,72,1792]{3,2,1,0:T(8,128)(2,1)} %get-tuple-element.39) | copy-start | bytes 12386308
  128.0 4.4 %copy-start.44 = (bf16[640,1792]{1,0:T(8,128)(2,1)}, bf16[640,1792]{1,0:T(8,128)(2,1)S(1)}, u32[]{:S(2)}) copy-start(bf16[640,1792]{1,0:T(8,128)(2,1)S(1)} %get-tuple-element.100) | copy-start | bytes 6881284
  171.4 10.5 %copy-start.37 = (bf16[4,4,72,1792]{3,2,1,0:T(8,128)(2,1)S(1)}, bf16[4,4,72,1792]{3,2,1,0:T(8,128)(2,1)}, u32[]{:S(2)}) copy-start(bf16[4,4,72,1792]{3,2,1,0:T(8,128)(2,1)} %get-tuple-element.37) | copy-start | bytes 12386308
  181.8 3.2 copy-start.36
  185.0 4.3 %copy-start.41 = (bf16[4,160,1152]{2,1,0:T(8,128)(2,1)S(1)}, bf16[4,160,1152]{2,1,0:T(8,128)(2,1)}, u32[]{:S(2)}) copy-start(bf16[4,160,1152]{2,1,0:T(8,128)(2,1)} %get-tuple-element.36) | copy-start | bytes 4423684
  194.7 5.3 %copy-start.42 = (bf16[4,160,1152]{2,1,0:T(8,128)(2,1)S(1)}, bf16[4,160,1152]{2,1,0:T(8,128)(2,1)}, u32[]{:S(2)}) copy-start(bf16[4,160,1152]{2,1,0:T(8,128)(2,1)} %get-tuple-element.42) | copy-start | bytes 4423684
  194.7 5.3 %copy-start.45 = (bf16[640,1792]{1,0:T(8,128)(2,1)S(1)}, bf16[640,1792]{1,0:T(8,128)(2,1)}, u32[]{:S(2)}) copy-start(bf16[640,1792]{1,0:T(8,128)(2,1)} %copy-done.44) | copy-start | bytes 6881284
  254.3 2.2 copy-start.8
  257.0 0.9 copy-start.15
  257.0 1.0 copy-start.16
  257.0 1.4 copy-start.12
  257.0 1.4 copy-start.14
  257.0 1.9 copy-start.34
  258.0 2.5 copy-start.3
  258.0 2.5 copy-start.28
  258.9 2.3 copy-start.4
  263.9 2.0 copy-start.6
  263.9 2.7 copy-start.39
  267.3 1.5 copy-start.25
  267.3 1.5 copy-start.26
  267.3 1.6 copy-start.31
  267.3 1.8 copy-start.32
  273.0 43.1 %copy-start = (bf16[160,1152]{1,0:T(8,128)(2,1)S(1)}, bf16[160,1152]{1,0:T(8,128)(2,1)}, u32[]{:S(2)}) copy-start(bf16[160,1152]{1,0:T(8,128)(2,1)} %tokens.7) | copy-start | bytes 1105924
  273.0 44.7 %copy-start.9 = (f32[160,1152]{1,0:T(8,128)S(1)}, f32[160,1152]{1,0:T(8,128)}, u32[]{:S(2)}) copy-start(f32[160,1152]{1,0:T(8,128)} %get-tuple-element.43) | copy-start | bytes 2211844
  316.0 5.5 %copy-start.21 = (f32[72,768]{1,0:T(8,128)S(1)}, f32[72,768]{1,0:T(8,128)}, u32[]{:S(2)}) copy-start(f32[72,768]{1,0:T(8,128)} %get-tuple-element.49) | copy-start | bytes 663556
  316.0 6.1 %copy-start.20 = (bf16[72,1792]{1,0:T(8,128)(2,1)S(1)}, bf16[72,1792]{1,0:T(8,128)(2,1)}, u32[]{:S(2)}) copy-start(bf16[72,1792]{1,0:T(8,128)(2,1)} %get-tuple-element.50) | copy-start | bytes 774148
  316.2 6.8 %copy-start.19 = (bf16[72,1792]{1,0:T(8,128)(2,1)S(1)}, bf16[72,1792]{1,0:T(8,128)(2,1)}, u32[]{:S(2)}) copy-start(bf16[72,1792]{1,0:T(8,128)(2,1)} %get-tuple-element.51) | copy-start | bytes 774148
  317.7 6.1 %copy-start.18 = (bf16[72,1792]{1,0:T(8,128)(2,1)S(1)}, bf16[72,1792]{1,0:T(8,128)(2,1)}, u32[]{:S(2)}) copy-start(bf16[72,1792]{1,0:T(8,128)(2,1)} %get-tuple-element.52) | copy-start | bytes 774148
  317.7 8.3 %copy-start.17 = (bf16[160,1152]{1,0:T(8,128)(2,1)S(1)}, bf16[160,1152]{1,0:T(8,128)(2,1)}, u32[]{:S(2)}) copy-start(bf16[160,1152]{1,0:T(8,128)(2,1)} %get-tuple-element.122) | copy-start | bytes 1105924

commit v2 on v1

--- a/solution.py
+++ b/solution.py
@@ -154,17 +154,27 @@
     )
 
 
+def merge(streams):
+    waiting = []
+
+    def advance(stream, k):
+        try:
+            waiting.append((next(stream), k, stream))
+        except StopIteration:
+            pass
+
+    for k, stream in enumerate(streams):
+        advance(stream, k)
+    while waiting:
+        waiting.sort(key=lambda entry: entry[:2])
+        yield waiting[0][0]
+        _, k, stream = waiting.pop(0)
+        advance(stream, k)
+
+
 def run_streams(streams):
-    streams = list(streams)
-    while streams:
-        alive = []
-        for stream in streams:
-            try:
-                next(stream)
-                alive.append(stream)
-            except StopIteration:
-                pass
-        streams = alive
+    for _ in merge(streams):
+        pass
 
 
 def halves(n):
@@ -199,7 +209,7 @@
 def merge_own(place, own, other, both, send, recv):
     copy = remote(own, other, send, recv, place.partner())
     copy.start()
-    yield
+    yield 2
     copy.wait()
     mine = own[...].astype(F32)
     theirs = other[...].astype(F32)
@@ -209,7 +219,7 @@
     ).astype(BF16)
 
 
-def gather_half(ax, both, out, ring_send, ring_recv, chip_send, chip_recv):
+def gather_half(ax, both, out, base, ring_send, ring_recv, chip_send, chip_recv):
     place, s = ax.place, ax.place.s
     cols = ax.mine
     sent = []
@@ -235,32 +245,32 @@
     send(own, ax.u, ax.v, ax.device(u=wrap(ax.u + s)), 0)
     send(own, ax.u, ax.v, ax.device(u=wrap(ax.u - s)), 1)
     along_v(own, ax.u, 0)
-    yield
+    yield base + 3
     arrive(us[1], ax.v, 0)
     src = ax.chunk(out, us[1], ax.v, cols)
     send(src, us[1], ax.v, ax.device(u=wrap(ax.u + s)), 2)
     along_v(src, us[1], 1)
-    yield
+    yield base + 3
     arrive(us[2], ax.v, 1)
     along_v(ax.chunk(out, us[2], ax.v, cols), us[2], 2)
-    yield
+    yield base + 5
     for r in range(4):
         if r == 1:
             arrive(us[3], ax.v, 2)
             along_v(ax.chunk(out, us[3], ax.v, cols), us[3], 3)
-            yield
+            yield base + 6
         v = wrap(ax.v - s)
         arrive(us[r], v, 3 + 3 * r)
         send(ax.chunk(out, us[r], v, cols), us[r], v, ax.device(v=wrap(ax.v + s)), 5 + 3 * r)
-        yield
+        yield base + 4.5 + 2.5 * r
         arrive(us[r], wrap(ax.v + s), 4 + 3 * r)
-        yield
+        yield base + (5 if r == 0 else 4 + 2.5 * (r + 1))
     for r in range(4):
         arrive(us[r], wrap(ax.v + 2), 5 + 3 * r)
-        yield
+        yield base + 14 + r
+    yield 90
     for copy in sent:
         copy.wait_send()
-    yield
     theirs = [ax.u, wrap(ax.u + s), wrap(ax.u - s), wrap(ax.u + 2)]
     landing = [(theirs[1], ax.v), (theirs[2], ax.v), (theirs[3], ax.v)]
     for r in range(4):
@@ -270,28 +280,22 @@
         remote(here, here, chip_send.at[k], chip_recv.at[k], place.partner()).wait_recv()
 
 
-def gather_stream(place, own, out, scratch):
+def gather_stream(place, own, out, scratch, base=0):
     other, both, sems, local = scratch
     n = own.shape[1]
     yield from merge_own(place, own, other, both, sems.at[0, 0, 0, 15], sems.at[0, 0, 1, 15])
     keep = pltpu.make_async_copy(both, out.at[place.y, place.x], local)
     keep.start()
-    parts = [
-        gather_half(
-            Axes(place, h, n), both, out, sems.at[h, 0, 0], sems.at[h, 0, 1], sems.at[h, 1, 0], sems.at[h, 1, 1]
-        )
-        for h in (0, 1)
-    ]
-    while parts:
-        alive = []
-        for part in parts:
-            try:
-                next(part)
-                alive.append(part)
-            except StopIteration:
-                pass
-        parts = alive
-        yield
+    yield base + 2
+    yield from merge(
+        [
+            gather_half(
+                Axes(place, h, n), both, out, base + 2,
+                sems.at[h, 0, 0], sems.at[h, 0, 1], sems.at[h, 1, 0], sems.at[h, 1, 1],
+            )
+            for h in (0, 1)
+        ]
+    )
     keep.wait()
 
 
@@ -318,12 +322,13 @@
         lax.fori_loop(0, count, body, 0)
 
 
-def scatter_half(ax, grads, final, bufs, sems):
+def scatter_half(ax, grads, final, bufs, sems, base):
     held, got, b1, b2, b3, c1, c2, c3, total = bufs
     place, s = ax.place, ax.place.s
     vs = [wrap(ax.v + 2), wrap(ax.v - s), wrap(ax.v + s), ax.v]
     for_partner = [wrap(ax.v + 2), wrap(ax.v + s), wrap(ax.v - s), ax.v]
     sent, loads, gets = [], [], []
+    yield base
     for k in range(4):
         give = remote(
             ax.group(grads, for_partner[k], ax.theirs),
@@ -338,7 +343,7 @@
         load = pltpu.make_async_copy(ax.group(grads, vs[k], ax.mine), held.at[k], sems.at[2, k])
         load.start()
         loads.append(load)
-    yield
+    yield base + 3
 
     def chip_sum(k):
         loads[k].wait()
@@ -353,20 +358,20 @@
 
     chip_sum(0)
     far = send(got.at[0], b1, 4, ax.device(v=wrap(ax.v + s)))
-    yield
+    yield base + 4
     chip_sum(1)
     back = send(got.at[1], b2, 5, ax.device(v=wrap(ax.v - s)))
-    yield
+    yield base + 6
     chip_sum(2)
-    yield
+    yield base + 8
     far.wait_recv()
     add_chunks(4, lambda i: b1.at[i], lambda i: b1.at[i], lambda i: got.at[2, i])
     forth = send(b1, b3, 6, ax.device(v=wrap(ax.v + s)))
-    yield
+    yield base + 9
     loads[3].wait()
     gets[3].wait_recv()
     back.wait_recv()
-    yield
+    yield base + 13
     forth.wait_recv()
     add_chunks(
         4,
@@ -378,18 +383,18 @@
     )
     far = send(total.at[wrap(ax.u + 2)], c1, 7, ax.device(u=wrap(ax.u + s)))
     back = send(total.at[wrap(ax.u - s)], c2, 8, ax.device(u=wrap(ax.u - s)))
-    yield
+    yield base + 17
     far.wait_recv()
     add_chunks(1, lambda i: c1, lambda i: c1, lambda i: total.at[wrap(ax.u + s)])
     forth = send(c1, c3, 9, ax.device(u=wrap(ax.u + s)))
-    yield
+    yield base + 21
     back.wait_recv()
     forth.wait_recv()
     add_chunks(1, lambda i: c2, lambda i: total.at[ax.u], lambda i: c2, lambda i: c3)
     keep = pltpu.make_async_copy(c2, final.at[:, ax.mine], sems.at[2, 4])
     keep.start()
     last = send(c2, final.at[:, ax.mine], 10, place.partner())
-    yield
+    yield 90
     for copy in sent:
         copy.wait_send()
     keep.wait()
@@ -407,14 +412,14 @@
     return shapes
 
 
-def scatter_streams(place, grads, final, scratch):
+def scatter_streams(place, grads, final, scratch, base=0):
     n = grads.shape[3]
     for h in (0, 1):
         part = scratch[10 * h : 10 * h + 10]
-        yield scatter_half(Axes(place, h, n), grads, final, part[:9], part[9])
-
-
-def rows_gather(place, out, sems):
+        yield scatter_half(Axes(place, h, n), grads, final, part[:9], part[9], base)
+
+
+def rows_gather(place, out, sems, base=0):
     s, z = place.s, place.z
     ahead, behind = place.device(z=wrap(z + s)), place.device(z=wrap(z - s))
 
@@ -425,14 +430,13 @@
     first.start()
     second = copy(z, 1, behind)
     second.start()
-    yield
+    yield base + 9
     copy(wrap(z - s), 0, ahead).wait_recv()
     relay = copy(wrap(z - s), 2, ahead)
     relay.start()
-    yield
+    yield base + 9.5
     copy(wrap(z + s), 1, ahead).wait_recv()
-    yield
-    yield
+    yield base + 14
     copy(wrap(z + 2), 2, ahead).wait_recv()
     for sent in (first, second, relay):
         sent.wait_send()
@@ -450,8 +454,7 @@
     far.start()
     back = copy(parts.at[wrap(z - s)], b2, 1, behind)
     back.start()
-    yield
-    yield
+    yield 9
     far.wait_recv()
     mid = wrap(z + s)
 
@@ -463,9 +466,9 @@
     lax.fori_loop(0, ROWS // 32, body, 0)
     forth = copy(b1, b3, 2, ahead)
     forth.start()
-    yield
+    yield 10
     back.wait_recv()
-    yield
+    yield 15
     forth.wait_recv()
     for sent in (far, back, forth):
         sent.wait_send()
@@ -487,7 +490,7 @@
     ref[8 * row : 8 * row + 8, :] = ref[8 * row : 8 * row + 8, :] + values[:8] + values[8:]
 
 
-def start_kernel(tokens, attn_own, rows_out, mats_out, sems, *scratch):
+def start_kernel(tokens, attn_own, own_g, rows_out, mats_out, full_g, sems, *scratch):
     place = Place()
     place.greet(True)
 
@@ -495,10 +498,16 @@
         rows_out[place.z] = tokens[...]
         yield from rows_gather(place, rows_out, sems)
 
-    run_streams([gather_stream(place, attn_own, mats_out, scratch), z_stream()])
-
-
-def middle_kernel(parts, tokens, gains, own_g, own_u, own_d, rows_out, attn_sum, full_g, full_u, full_d, *scratch):
+    run_streams(
+        [
+            gather_stream(place, attn_own, mats_out, scratch[:4]),
+            gather_stream(place, own_g, full_g, scratch[4:8], 6),
+            z_stream(),
+        ]
+    )
+
+
+def middle_kernel(parts, tokens, gains, own_u, own_d, rows_out, attn_sum, full_u, full_d, *scratch):
     place = Place()
     place.greet(True)
     b1, b2, b3, sems, sems2 = scratch[:5]
@@ -517,19 +526,20 @@
             rows_out[place.z, rows, :] = (mid * gains[2:3, :]).astype(BF16)
 
         row_blocks(body)
-        yield from rows_gather(place, rows_out, sems2)
+        yield from rows_gather(place, rows_out, sems2, 17)
 
     run_streams(
         [
             z_stream(),
-            gather_stream(place, own_g, full_g, scratch[5:9]),
-            gather_stream(place, own_u, full_u, scratch[9:13]),
-            gather_stream(place, own_d, full_d, scratch[13:17]),
+            gather_stream(place, own_u, full_u, scratch[5:9]),
+            gather_stream(place, own_d, full_d, scratch[9:13], 9),
         ]
     )
 
 
-def turn_kernel(parts, tokens, attn_sum, gains, cotangent, rows_out, layer_out, sums, *scratch):
+def turn_kernel(
+    parts, tokens, attn_sum, gains, cotangent, gate, upward, rows_out, layer_out, sums, by_gate, by_up, *scratch
+):
     place = Place()
     place.greet(False)
     b1, b2, b3, sems, sems2 = scratch[:5]
@@ -551,14 +561,52 @@
             rows_out[place.z, rows, :] = normalize_back(grad * gains[3:4, :], hat, inverse).astype(BF16)
 
         row_blocks(body)
-        yield from rows_gather(place, rows_out, sems2)
-
-    run_streams([z_stream()])
+        yield from rows_gather(place, rows_out, sems2, 17)
+
+    held_g, held_u, moves = scratch[5:8]
+
+    def gelu_stream():
+        def load(i):
+            return (
+                pltpu.make_async_copy(gate.at[i], held_g.at[i], moves.at[0, i]),
+                pltpu.make_async_copy(upward.at[i], held_u.at[i], moves.at[1, i]),
+            )
+
+        def store(i):
+            return (
+                pltpu.make_async_copy(held_g.at[i], by_gate.at[i], moves.at[0, i]),
+                pltpu.make_async_copy(held_u.at[i], by_up.at[i], moves.at[1, i]),
+            )
+
+        for i in range(8):
+            for copy in load(i):
+                copy.start()
+        for i in range(8):
+            yield (1 + i if i < 4 else 7 + i)
+            for copy in load(i):
+                copy.wait()
+
+            def step(k, carry):
+                rows = pl.ds(pl.multiple_of(k * 8, 8), 8)
+                value, slope = gelu_parts(held_g[i, rows, :])
+                held_g[i, rows, :] = held_u[i, rows, :] * slope
+                held_u[i, rows, :] = value
+                return carry
+
+            lax.fori_loop(0, 10, step, 0)
+            for copy in store(i):
+                copy.start()
+        yield 80
+        for i in range(8):
+            for copy in store(i):
+                copy.wait()
+
+    run_streams([z_stream(), gelu_stream()])
 
 
 def back_kernel(
-    parts, tokens, attn_sum, gains, cotangent, grad_g, grad_u, grad_d,
-    rows_out, grad_hidden, sums, sum_g, sum_u, sum_d, *scratch
+    parts, tokens, attn_sum, gains, cotangent, grad_d, grad_g,
+    rows_out, grad_hidden, sums, sum_d, sum_g, *scratch
 ):
     place = Place()
     place.greet(True)
@@ -584,15 +632,15 @@
             ).astype(BF16)
 
         row_blocks(body)
-        yield from rows_gather(place, rows_out, sems2)
+        yield from rows_gather(place, rows_out, sems2, 17)
 
     streams = [z_stream()]
-    for i, (grads, final) in enumerate(((grad_d, sum_d), (grad_g, sum_g), (grad_u, sum_u))):
-        streams += list(scatter_streams(place, grads, final, scratch[5 + 20 * i : 25 + 20 * i]))
+    for i, (grads, final) in enumerate(((grad_d, sum_d), (grad_g, sum_g))):
+        streams += list(scatter_streams(place, grads, final, scratch[5 + 20 * i : 25 + 20 * i], 9 * i))
     run_streams(streams)
 
 
-def end_kernel(parts, grads, grad_rows, final, shared, *scratch):
+def end_kernel(parts, grads, grad_u, grad_rows, final, shared, sum_u, *scratch):
     place = Place()
     place.greet(True, far_z=True)
     b1, b2, b3, sems, sems2 = scratch[:5]
@@ -608,21 +656,25 @@
 
         row_blocks(body)
 
-    run_streams([z_stream()] + list(scatter_streams(place, grads, final, scratch[8:28])))
-    cols = pl.ds(512, 768)
-    copies = []
-    for k in range(3):
-        copy = remote(
-            final.at[:, cols], got.at[k], zsend.at[k], zrecv.at[k], place.device(z=wrap(place.z + k + 1))
-        )
-        copy.start()
-        copies.append(copy)
-    for copy in copies:
-        copy.wait()
-    total = final[:, cols].astype(F32)
-    for k in range(3):
-        total = total + got[k].astype(F32)
-    shared[...] = total
+    def attn_stream():
+        yield from merge(scatter_streams(place, grads, final, scratch[8:28]))
+        cols = pl.ds(512, 768)
+        copies = []
+        for k in range(3):
+            copy = remote(
+                final.at[:, cols], got.at[k], zsend.at[k], zrecv.at[k], place.device(z=wrap(place.z + k + 1))
+            )
+            copy.start()
+            copies.append(copy)
+        yield 95
+        for copy in copies:
+            copy.wait()
+        total = final[:, cols].astype(F32)
+        for k in range(3):
+            total = total + got[k].astype(F32)
+        shared[...] = total
+
+    run_streams([attn_stream(), z_stream()] + list(scatter_streams(place, grad_u, sum_u, scratch[28:48], 5)))
 
 
 def call(kernel, outs, ins, spaces, out_spaces, scratch, ident):
@@ -674,13 +726,14 @@
         + [jnp.zeros((shard, ATTN_COLS - 1024 - 6), BF16)],
         axis=1,
     )
-    tokens_all, mats = call(
+    whole = ((4, 4, CHUNK, FFPAD), BF16)
+    tokens_all, mats, full_gate = call(
         start_kernel,
-        [((4, ROWS, WIDTH), BF16), ((4, 4, CHUNK, ATTN_COLS), BF16)],
-        [tokens, attn_own],
-        [vm, vm],
-        [vm, hbm],
-        [pltpu.SemaphoreType.DMA((2, 3))] + gather_scratch(ATTN_COLS),
+        [((4, ROWS, WIDTH), BF16), ((4, 4, CHUNK, ATTN_COLS), BF16), whole],
+        [tokens, attn_own, jnp.pad(w_gate, pad)],
+        [vm, vm, vm],
+        [vm, hbm, hbm],
+        [pltpu.SemaphoreType.DMA((2, 3))] + gather_scratch(ATTN_COLS) + gather_scratch(FFPAD),
         0,
     )
     mats = mats.reshape(WIDTH, ATTN_COLS)
@@ -704,21 +757,19 @@
     piece, logsum = attend_forward(queries, keys, values, mask, scale)
     heads_out = piece.astype(BF16)
     attn_part = contract_cols(heads_out, full_out).astype(BF16)
-    whole = ((4, 4, CHUNK, FFPAD), BF16)
-    ffw_rows, attn_sum, full_gate, full_up, full_down = call(
+    ffw_rows, attn_sum, full_up, full_down = call(
         middle_kernel,
-        [((4, ROWS, WIDTH), BF16), ((ROWS, WIDTH), F32), whole, whole, whole],
+        [((4, ROWS, WIDTH), BF16), ((ROWS, WIDTH), F32), whole, whole],
         [
             attn_part.reshape(4, ROWS, WIDTH),
             tokens,
             gains,
-            jnp.pad(w_gate, pad),
             jnp.pad(w_up, pad),
             jnp.pad(w_down.T, pad),
         ],
-        [vm] * 6,
-        [vm, vm, hbm, hbm, hbm],
-        rows_scratch() + gather_scratch(FFPAD) * 3,
+        [vm] * 5,
+        [vm, vm, hbm, hbm],
+        rows_scratch() + gather_scratch(FFPAD) * 2,
         1,
     )
     ffw_rows = ffw_rows.reshape(4 * ROWS, WIDTH)
@@ -727,44 +778,52 @@
     full_down = full_down.reshape(WIDTH, FFPAD)
     gate = jnp.dot(ffw_rows, full_gate, preferred_element_type=F32)
     upward = jnp.dot(ffw_rows, full_up, preferred_element_type=F32)
-    gelu_value, gelu_slope = gelu_parts(gate)
+    gelu_value, _ = gelu_parts(gate)
     act = (gelu_value * upward).astype(BF16)
     ffw_part = contract_cols(act, full_down).astype(BF16)
-    grad_ffw, layer_out, ffw_sums = call(
+    blocks = (8, 80, FFPAD)
+    grad_ffw, layer_out, ffw_sums, by_gate, by_up = call(
         turn_kernel,
-        [((4, ROWS, WIDTH), BF16), ((ROWS, WIDTH), BF16), ((8, WIDTH), F32)],
-        [ffw_part.reshape(4, ROWS, WIDTH), tokens, attn_sum, gains, cotangent],
-        [vm] * 5,
-        [vm] * 3,
-        rows_scratch(),
+        [((4, ROWS, WIDTH), BF16), ((ROWS, WIDTH), BF16), ((8, WIDTH), F32), (blocks, F32), (blocks, F32)],
+        [
+            ffw_part.reshape(4, ROWS, WIDTH),
+            tokens,
+            attn_sum,
+            gains,
+            cotangent,
+            gate.reshape(blocks),
+            upward.reshape(blocks),
+        ],
+        [vm] * 5 + [hbm] * 2,
+        [vm] * 3 + [hbm] * 2,
+        rows_scratch() + [pltpu.VMEM(blocks, F32)] * 2 + [pltpu.SemaphoreType.DMA((2, 8))],
         2,
     )
     grad_ffw = grad_ffw.reshape(4 * ROWS, WIDTH)
     grad_down = contract_rows(grad_ffw, act).astype(BF16)
     grad_act = jnp.dot(grad_ffw, full_down, preferred_element_type=F32)
-    grad_gate_in = (grad_act * upward * gelu_slope).astype(BF16)
-    grad_up_in = (grad_act * gelu_value).astype(BF16)
+    grad_gate_in = (grad_act * by_gate.reshape(4 * ROWS, FFPAD)).astype(BF16)
+    grad_up_in = (grad_act * by_up.reshape(4 * ROWS, FFPAD)).astype(BF16)
     grad_gate = contract_rows(ffw_rows, grad_gate_in).astype(BF16)
     grad_up = contract_rows(ffw_rows, grad_up_in).astype(BF16)
     mid_part = (contract_cols(grad_gate_in, full_gate) + contract_cols(grad_up_in, full_up)).astype(BF16)
     split = (4, 4, CHUNK, FFPAD)
     final = ((CHUNK, FFPAD), BF16)
-    grad_attn, grad_hidden, mid_sums, sum_gate, sum_up, sum_down = call(
+    grad_attn, grad_hidden, mid_sums, sum_down, sum_gate = call(
         back_kernel,
-        [((4, ROWS, WIDTH), BF16), ((ROWS, WIDTH), F32), ((16, WIDTH), F32), final, final, final],
+        [((4, ROWS, WIDTH), BF16), ((ROWS, WIDTH), F32), ((16, WIDTH), F32), final, final],
         [
             mid_part.reshape(4, ROWS, WIDTH),
             tokens,
             attn_sum,
             gains,
             cotangent,
+            grad_down.reshape(split),
             grad_gate.reshape(split),
-            grad_up.reshape(split),
-            grad_down.reshape(split),
         ],
-        [vm] * 5 + [hbm] * 3,
-        [vm] * 6,
-        rows_scratch() + scatter_scratch(FFPAD) * 3,
+        [vm] * 5 + [hbm] * 2,
+        [vm] * 5,
+        rows_scratch() + scatter_scratch(FFPAD) * 2,
         3,
     )
     grad_attn = grad_attn.reshape(4 * ROWS, WIDTH)
@@ -805,19 +864,24 @@
     grads = jnp.concatenate(
         [g.astype(BF16) for g in (grad_query, grad_output, grad_key, grad_value, small_grads)], axis=1
     )
-    grad_in_rows, sum_attn, sum_shared = call(
+    grad_in_rows, sum_attn, sum_shared, sum_up = call(
         end_kernel,
-        [((ROWS, WIDTH), F32), ((CHUNK, ATTN_COLS), BF16), ((CHUNK, ATTN_COLS - 512), F32)],
-        [in_part.astype(BF16).reshape(4, ROWS, WIDTH), grads.reshape(4, 4, CHUNK, ATTN_COLS)],
-        [vm, hbm],
-        [vm] * 3,
+        [((ROWS, WIDTH), F32), ((CHUNK, ATTN_COLS), BF16), ((CHUNK, ATTN_COLS - 512), F32), final],
+        [
+            in_part.astype(BF16).reshape(4, ROWS, WIDTH),
+            grads.reshape(4, 4, CHUNK, ATTN_COLS),
+            grad_up.reshape(split),
+        ],
+        [vm, hbm, hbm],
+        [vm] * 4,
         rows_scratch()
         + [
             pltpu.VMEM((3, CHUNK, ATTN_COLS - 512), BF16),
             pltpu.SemaphoreType.DMA((3,)),
             pltpu.SemaphoreType.DMA((3,)),
         ]
-        + scatter_scratch(ATTN_COLS),
+        + scatter_scratch(ATTN_COLS)
+        + scatter_scratch(FFPAD),
         4,
     )
     normed_in, inverse_in = normalize(tokens.astype(F32))

time: 332 us -> 337 us (1.015)
  local copies, waits for them, and re-layouts: 19.9 us -> 27.5 us
  Pallas kernels: 219 us -> 213 us
  matrix products: 70.9 us -> 75.4 us
    dot_general x9, matrix products: 19.8 us -> 27.1 us  [contract_rows(): lax.dot_general(left, right, (((0,), (0,)), ((), ())), preferred_element_...]
    pallas_call x5, Pallas kernels: 219 us -> 213 us  [call(): pl.pallas_call(kernel, out_shape=[jax.ShapeDtypeStruct(shape, dtype) for...]
where the time goes in v2:
time: 337 us; the launch traced here: 331 us
  Pallas kernels  213 us (63%)
  matrix products  75.4 us (22%)
  local copies, waits for them, and re-layouts  27.5 us (8%)
  other arithmetic  13.4 us (4%)
    pallas_call x5, Pallas kernels, call(): pl.pallas_call(kernel, out_shape=[jax.ShapeDtypeStruct(shape, dtype) for...  213 us
    dot_general x9, matrix products, contract_rows(): lax.dot_general(left, right, (((0,), (0,)), ((), ())), preferred_element_...  27.1 us
    dot_general x9, matrix products, contract_cols(): lax.dot_general(left, right, (((1,), (1,)), ((), ())), preferred_element_...  20 us
    dot_general x1, matrix products, local(): grad_act = jnp.dot(grad_ffw, full_down, preferred_element_type=F32)  8.52 us

profile of v2, /device:TPU:0, one launch (start us, length us, event | category | flops | bytes accessed | tf_op | source)
XLA Modules:
  0.0 331.1 jit_solution(9734016394141145618)
XLA Ops:
  0.6 0.7 pad_bitcast_fusion.1
  1.4 0.7 pad_bitcast_fusion
  2.2 0.8 copy.40
  3.0 0.8 copy.41
  3.7 0.8 copy.42
  4.5 0.8 copy.43
  5.3 1.5 concatenate.20.attn_own
  6.8 1.6 pad.33.own_g
  8.4 41.6 %start_kernel.1 = (bf16[4,160,1152]{2,1,0:T(8,128)(2,1)}, bf16[4,4,72,1280]{3,2,1,0:T(8,128)(2,1)}, bf16[4,4,72,1792]{3,2,1,0:T(8,128)(2,1)}) custom-call(bf16[160,1152]{1,0:T(8,128)(2,1)} %tokens.7, bf16[36,1280]{1,0:T(8,128)(2,1)} %concatenate.20.attn_own, bf16[36,1792]{1,0:T(8,128)(2,1)} %pad.33.own_g), custom_call_target="tpu_custom_call" | custom-call | tf_op jit(solution)/shard_map/start_kernel/pallas_call | solution.py:681
  50.0 1.1 slice.191
  51.3 1.7 multiply_reduce_fusion.1
  53.5 2.2 multiply_reduce_fusion.8
  55.8 2.0 multiply_reduce_fusion.7
  58.6 2.3 fusion.58
  61.0 1.7 fusion.78
  62.9 1.7 convolution_convert_fusion.12
  64.6 0.7 copy-done.17
  65.3 0.5 convolution_convert_fusion.11
  65.8 2.8 convolution_convert_fusion.3
  68.6 0.7 pad.34.own_u
  69.3 0.7 pad.35.own_d
  70.0 43.9 %middle_kernel.1 = (bf16[4,160,1152]{2,1,0:T(8,128)(2,1)}, f32[160,1152]{1,0:T(8,128)}, bf16[4,4,72,1792]{3,2,1,0:T(8,128)(2,1)}, bf16[4,4,72,1792]{3,2,1,0:T(8,128)(2,1)}) custom-call(bf16[4,160,1152]{2,1,0:T(8,128)(2,1)} %bitcast.93, bf16[160,1152]{1,0:T(8,128)(2,1)} %tokens.7, f32[8,1152]{1,0:T(8,128)} %copy-done.23, bf16[36,1792]{1,0:T(8,128)(2,1)} %pad.34.own_u, ...), custom_call_target="tpu_custom_call" | custom-call | tf_op jit(solution)/shard_map/middle_kernel/pallas_call | solution.py:681
  113.9 5.9 %fusion.79 = f32[640,1792]{1,0:T(8,128)S(1)} fusion(bf16[640,1152]{1,0:T(8,128)(2,1)} %bitcast.126, bf16[1152,1792]{1,0:T(8,128)(2,1)} %bitcast.122), kind=kOutput, calls=%fused_computation.156 | convolution fusion | flops 2642411520 | bytes 10190848 | tf_op jit(solution)/shard_map/dot_general | solution.py:779
  119.8 4.8 %fusion.5 = (bf16[640,1792]{1,0:T(8,128)(2,1)S(1)}, f32[640,1792]{1,0:T(8,128)}) fusion(f32[640,1792]{1,0:T(8,128)S(1)} %fusion.79, bf16[640,1152]{1,0:T(8,128)(2,1)S(1)} %bitcast.127, bf16[1152,1792]{1,0:T(8,128)(2,1)S(1)} %bitcast.124), kind=kOutput, calls=%fused_computation.9 | convolution fusion | flops 2653880320 | bytes 17072128 | tf_op jit(solution)/shard_map/dot_general | solution.py:780
  124.8 4.2 %convolution_convert_fusion.4 = bf16[640,1152]{1,0:T(8,128)(2,1)} fusion(bf16[640,1792]{1,0:T(8,128)(2,1)S(1)} %get-tuple-element.104, bf16[1152,1792]{1,0:T(8,128)(2,1)S(1)} %bitcast.100), kind=kOutput, calls=%fused_computation.19 | convolution fusion | flops 2643148800 | bytes 7897088 | tf_op jit(solution)/shard_map/dot_general | solution.py:76
  129.1 35.2 %turn_kernel.1 = (bf16[4,160,1152]{2,1,0:T(8,128)(2,1)}, bf16[160,1152]{1,0:T(8,128)(2,1)}, f32[8,1152]{1,0:T(8,128)}, f32[8,80,1792]{2,1,0:T(8,128)}, f32[8,80,1792]{2,1,0:T(8,128)}) custom-call(bf16[4,160,1152]{2,1,0:T(8,128)(2,1)} %bitcast.113, bf16[160,1152]{1,0:T(8,128)(2,1)} %tokens.7, f32[160,1152]{1,0:T(8,128)} %get-tuple-element.42.attn_sum, ...), custom_call_target="tpu_custom_call" | custom-call | tf_op jit(solution)/shard_map/turn_kernel/pallas_call | solution.py:681
  164.3 8.5 %fusion.6 = (bf16[640,1792]{1,0:T(8,128)(2,1)S(1)}, bf16[640,1792]{1,0:T(8,128)(2,1)S(1)}) fusion(f32[8,80,1792]{2,1,0:T(8,128)} %get-tuple-element.46, f32[8,80,1792]{2,1,0:T(8,128)} %get-tuple-element.45, bf16[640,1152]{1,0:T(8,128)(2,1)} %bitcast.110, bf16[1152,1792]{1,0:T(8,128)(2,1)} %bitcast.99), kind=kOutput, calls=%fused_computation.11 | convolution fusion | flops 2646999040 | bytes 19365888 | tf_op jit(solution)/shard_map/dot_general | solution.py:804
  172.8 5.4 %convolution_convert_fusion.1 = bf16[1152,1792]{1,0:T(8,128)(2,1)} fusion(bf16[640,1152]{1,0:T(8,128)(2,1)S(1)} %bitcast.128, bf16[640,1792]{1,0:T(8,128)(2,1)S(1)} %get-tuple-element.73), kind=kOutput, calls=%fused_computation.1 | convolution fusion | flops 2644475904 | bytes 7897088 | tf_op jit(solution)/shard_map/dot_general | solution.py:70
  178.2 5.4 %convolution_convert_fusion.2 = bf16[1152,1792]{1,0:T(8,128)(2,1)} fusion(bf16[640,1152]{1,0:T(8,128)(2,1)S(1)} %bitcast.111, bf16[640,1792]{1,0:T(8,128)(2,1)S(1)} %copy-done.46), kind=kOutput, calls=%fused_computation.2 | convolution fusion | flops 2644475904 | bytes 7897088 | tf_op jit(solution)/shard_map/dot_general | solution.py:70
  183.6 3.2 fusion.80
  186.8 4.3 %fusion.8 = bf16[640,1152]{1,0:T(8,128)(2,1)} fusion(f32[640,1152]{1,0:T(8,128)S(1)} %fusion.80, bf16[640,1792]{1,0:T(8,128)(2,1)S(1)} %get-tuple-element.72, bf16[1152,1792]{1,0:T(8,128)(2,1)S(1)} %bitcast.125), kind=kOutput, calls=%fused_computation.18 | convolution fusion | flops 2643886080 | bytes 10846208 | tf_op jit(solution)/shard_map/dot_general | solution.py:76
  191.1 47.4 %back_kernel.1 = (bf16[4,160,1152]{2,1,0:T(8,128)(2,1)}, f32[160,1152]{1,0:T(8,128)}, f32[16,1152]{1,0:T(8,128)}, bf16[72,1792]{1,0:T(8,128)(2,1)}, bf16[72,1792]{1,0:T(8,128)(2,1)}) custom-call(bf16[4,160,1152]{2,1,0:T(8,128)(2,1)} %bitcast.112, bf16[160,1152]{1,0:T(8,128)(2,1)} %tokens.7, f32[160,1152]{1,0:T(8,128)} %get-tuple-element.42.attn_sum, ...), custom_call_target="tpu_custom_call" | custom-call | tf_op jit(solution)/shard_map/back_kernel/pallas_call | solution.py:681
  238.5 1.7 fusion.74
  240.2 1.7 convert_bitcast_fusion
  241.9 2.1 convolution_convert_fusion.10
  244.1 0.4 convolution_convert_fusion.9
  244.5 0.5 multiply_reduce_fusion.2
  245.5 0.5 copy-done.28
  246.1 0.5 fusion.67
  246.6 0.5 fusion.68
  247.0 1.5 fusion.55
  249.4 0.7 copy-done.21
  250.1 0.8 copy-done.10
  250.9 0.6 fusion.32
  251.5 0.7 convolution_add_fusion.1
  252.2 2.1 multiply_reduce_fusion
  254.9 2.5 fusion.11
  257.4 2.9 fusion.9
  260.4 1.5 fusion.12
  261.9 1.5 fusion.10
  263.4 0.9 bitcast_dynamic-update-slice_fusion
  264.3 5.8 %copy.47 = bf16[1152,1280]{1,0:T(8,128)(2,1)} copy(bf16[1152,1280]{0,1:T(8,128)(2,1)} %bitcast_dynamic-update-slice_fusion) | data formatting | bytes 5898240 | tf_op jit(solution)/shard_map/concatenate | solution.py:864
  270.1 7.0 %convolution_convert_fusion = bf16[1152,1792]{1,0:T(8,128)(2,1)} fusion(bf16[640,1152]{1,0:T(8,128)(2,1)S(1)} %bitcast.129, bf16[640,1792]{1,0:T(8,128)(2,1)} %copy-done.8), kind=kOutput, calls=%fused_computation | convolution fusion | flops 2644475904 | bytes 7897088 | tf_op jit(solution)/shard_map/dot_general | solution.py:70
  277.1 45.2 %end_kernel.1 = (f32[160,1152]{1,0:T(8,128)}, bf16[72,1280]{1,0:T(8,128)(2,1)}, f32[72,768]{1,0:T(8,128)}, bf16[72,1792]{1,0:T(8,128)(2,1)}) custom-call(bf16[4,160,1152]{2,1,0:T(8,128)(2,1)} %bitcast.92, bf16[4,4,72,1280]{3,2,1,0:T(8,128)(2,1)} %bitcast.91, bf16[4,4,72,1792]{3,2,1,0:T(8,128)(2,1)} %bitcast.98), custom_call_target="tpu_custom_call" | custom-call | tf_op jit(solution)/shard_map/end_kernel/pallas_call | solution.py:681
  322.3 1.1 fusion.75
  323.4 0.7 fusion.69
  324.2 0.7 fusion.70
  325.4 1.1 fusion.23
  326.6 0.6 fusion.77
  327.2 0.9 select_convert_fusion
  328.1 0.6 slice_bitcast_fusion
  328.7 0.7 slice_reduce_fusion.2
  329.5 0.7 slice_reduce_fusion.9
  330.2 0.7 copy.54
  (137 shorter events, 4.5 us)
Async XLA Ops:
  49.9 3.2 copy-start.1
  51.2 4.6 %copy-start.23 = (f32[8,1152]{1,0:T(8,128)}, f32[8,1152]{1,0:T(8,128)S(1)}, u32[]{:S(2)}) copy-start(f32[8,1152]{1,0:T(8,128)S(1)} %convert_bitcast_fusion.1.gains) | copy-start | bytes 110596
  53.5 4.4 %copy-start.12 = (bf16[640,1152]{1,0:T(8,128)(2,1)}, bf16[640,1152]{1,0:T(8,128)(2,1)S(1)}, u32[]{:S(2)}) copy-start(bf16[640,1152]{1,0:T(8,128)(2,1)S(1)} %multiply_convert_fusion) | copy-start | bytes 4423684
  55.8 2.7 copy-start.2
  55.8 2.7 copy-start.38
  57.9 3.0 copy-start.4
  58.3 2.6 copy-start.37
  60.9 1.7 copy-start.24
  60.9 1.7 copy-start.26
  60.9 2.0 copy-start.13
  64.6 0.7 copy-start.17
  65.3 3.3 copy-start.33
  65.3 4.0 %copy-start.34 = (bf16[1728,36]{0,1:T(8,128)(2,1)S(1)}, bf16[1728,36]{0,1:T(8,128)(2,1)}, u32[]{:S(2)}) copy-start(bf16[1728,36]{0,1:T(8,128)(2,1)} %param.27) | copy-start | bytes 373252
  113.9 5.9 %copy-start.40 = (bf16[4,4,72,1792]{3,2,1,0:T(8,128)(2,1)S(1)}, bf16[4,4,72,1792]{3,2,1,0:T(8,128)(2,1)}, u32[]{:S(2)}) copy-start(bf16[4,4,72,1792]{3,2,1,0:T(8,128)(2,1)} %get-tuple-element.40) | copy-start | bytes 12386308
  113.9 5.9 %copy-start.42 = (bf16[4,160,1152]{2,1,0:T(8,128)(2,1)S(1)}, bf16[4,160,1152]{2,1,0:T(8,128)(2,1)}, u32[]{:S(2)}) copy-start(bf16[4,160,1152]{2,1,0:T(8,128)(2,1)} %get-tuple-element.38) | copy-start | bytes 4423684
  119.8 4.8 %copy-start.6 = (f32[640,1792]{1,0:T(8,128)}, f32[640,1792]{1,0:T(8,128)S(1)}, u32[]{:S(2)}) copy-start(f32[640,1792]{1,0:T(8,128)S(1)} %fusion.79) | copy-start | bytes 13762564
  119.8 5.0 %copy-start.7 = (bf16[4,4,72,1792]{3,2,1,0:T(8,128)(2,1)S(1)}, bf16[4,4,72,1792]{3,2,1,0:T(8,128)(2,1)}, u32[]{:S(2)}) copy-start(bf16[4,4,72,1792]{3,2,1,0:T(8,128)(2,1)} %get-tuple-element.41) | copy-start | bytes 12386308
  124.6 4.4 %copy-start.45 = (bf16[640,1792]{1,0:T(8,128)(2,1)}, bf16[640,1792]{1,0:T(8,128)(2,1)S(1)}, u32[]{:S(2)}) copy-start(bf16[640,1792]{1,0:T(8,128)(2,1)S(1)} %get-tuple-element.104) | copy-start | bytes 6881284
  164.2 8.6 %copy-start.43 = (bf16[4,160,1152]{2,1,0:T(8,128)(2,1)S(1)}, bf16[4,160,1152]{2,1,0:T(8,128)(2,1)}, u32[]{:S(2)}) copy-start(bf16[4,160,1152]{2,1,0:T(8,128)(2,1)} %get-tuple-element.38) | copy-start | bytes 4423684
  172.8 14.0 %copy-start.8 = (bf16[640,1792]{1,0:T(8,128)(2,1)}, bf16[640,1792]{1,0:T(8,128)(2,1)S(1)}, u32[]{:S(2)}) copy-start(bf16[640,1792]{1,0:T(8,128)(2,1)S(1)} %get-tuple-element.72) | copy-start | bytes 6881284
  172.8 5.4 %copy-start.11 = (bf16[4,160,1152]{2,1,0:T(8,128)(2,1)S(1)}, bf16[4,160,1152]{2,1,0:T(8,128)(2,1)}, u32[]{:S(2)}) copy-start(bf16[4,160,1152]{2,1,0:T(8,128)(2,1)} %get-tuple-element.44) | copy-start | bytes 4423684
  172.8 5.4 %copy-start.46 = (bf16[640,1792]{1,0:T(8,128)(2,1)S(1)}, bf16[640,1792]{1,0:T(8,128)(2,1)}, u32[]{:S(2)}) copy-start(bf16[640,1792]{1,0:T(8,128)(2,1)} %copy-done.45) | copy-start | bytes 6881284
  178.2 5.4 %copy-start.39 = (bf16[4,4,72,1792]{3,2,1,0:T(8,128)(2,1)S(1)}, bf16[4,4,72,1792]{3,2,1,0:T(8,128)(2,1)}, u32[]{:S(2)}) copy-start(bf16[4,4,72,1792]{3,2,1,0:T(8,128)(2,1)} %get-tuple-element.39) | copy-start | bytes 12386308
  183.6 3.2 copy-start.41
  241.9 2.6 copy-start.18
  244.5 7.6 %copy-start.15 = (bf16[640,256]{1,0:T(8,128)(2,1)}, bf16[640,256]{1,0:T(8,128)(2,1)S(1)}, u32[]{:S(2)}) copy-start(bf16[640,256]{1,0:T(8,128)(2,1)S(1)} %convolution_convert_fusion.9) | copy-start | bytes 983044
  245.1 0.9 copy-start.28
  245.1 1.0 copy-start.29
  245.1 1.4 copy-start.25
  245.1 1.4 copy-start.27
  246.6 2.0 copy-start.5
  247.0 1.9 copy-start.3
  248.8 2.1 copy-start.10
  249.0 2.5 copy-start.19
  249.4 0.7 copy-start.21
  252.2 2.6 copy-start.35
  252.2 2.6 copy-start.36
  252.2 2.7 copy-start.14
  254.9 5.4 %copy-start.20 = (bf16[640,256]{0,1:T(8,128)(2,1)S(1)}, bf16[640,256]{0,1:T(8,128)(2,1)}, u32[]{:S(2)}) copy-start(bf16[640,256]{0,1:T(8,128)(2,1)} %copy-done.19) | copy-start | bytes 983044
  257.4 4.5 %copy-start.16 = (bf16[640,256]{1,0:T(8,128)(2,1)S(1)}, bf16[640,256]{1,0:T(8,128)(2,1)}, u32[]{:S(2)}) copy-start(bf16[640,256]{1,0:T(8,128)(2,1)} %copy-done.15) | copy-start | bytes 983044
  264.3 5.8 %copy-start.44 = (bf16[4,160,1152]{2,1,0:T(8,128)(2,1)S(1)}, bf16[4,160,1152]{2,1,0:T(8,128)(2,1)}, u32[]{:S(2)}) copy-start(bf16[4,160,1152]{2,1,0:T(8,128)(2,1)} %get-tuple-element.38) | copy-start | bytes 4423684
  277.1 47.1 %copy-start.31 = (bf16[72,1792]{1,0:T(8,128)(2,1)S(1)}, bf16[72,1792]{1,0:T(8,128)(2,1)}, u32[]{:S(2)}) copy-start(bf16[72,1792]{1,0:T(8,128)(2,1)} %get-tuple-element.54) | copy-start | bytes 774148
  322.3 2.7 copy-start
  322.3 2.9 copy-start.9
  322.3 3.1 copy-start.22
  324.2 2.3 copy-start.32
  325.1 5.1 %copy-start.30 = (bf16[160,1152]{1,0:T(8,128)(2,1)S(1)}, bf16[160,1152]{1,0:T(8,128)(2,1)}, u32[]{:S(2)}) copy-start(bf16[160,1152]{1,0:T(8,128)(2,1)} %get-tuple-element.126) | copy-start | bytes 1105924

commit v3 on v2

--- a/solution.py
+++ b/solution.py
@@ -21,6 +21,10 @@
 FFPAD = 1792
 ATTN_COLS = 1280
 MESH = pl.DeviceIdType.MESH
+
+GATHER_AT = (4.5, 7.5, 7.0, 5.0, 5.0)
+SCATTER_AT = (4, 6, 8, 9, 13, 13.5, 20, 24, 27)
+ROWS_AT = (6, 10, 10.5, 12, 15)
 
 
 def normalize(inputs):
@@ -245,29 +249,30 @@
     send(own, ax.u, ax.v, ax.device(u=wrap(ax.u + s)), 0)
     send(own, ax.u, ax.v, ax.device(u=wrap(ax.u - s)), 1)
     along_v(own, ax.u, 0)
-    yield base + 3
+    yield base + GATHER_AT[0]
     arrive(us[1], ax.v, 0)
     src = ax.chunk(out, us[1], ax.v, cols)
     send(src, us[1], ax.v, ax.device(u=wrap(ax.u + s)), 2)
     along_v(src, us[1], 1)
-    yield base + 3
+    yield base + GATHER_AT[0] + 0.1
     arrive(us[2], ax.v, 1)
     along_v(ax.chunk(out, us[2], ax.v, cols), us[2], 2)
-    yield base + 5
+    yield base + GATHER_AT[2]
     for r in range(4):
         if r == 1:
+            yield base + GATHER_AT[1]
             arrive(us[3], ax.v, 2)
             along_v(ax.chunk(out, us[3], ax.v, cols), us[3], 3)
-            yield base + 6
+            yield base + GATHER_AT[2] + GATHER_AT[3]
         v = wrap(ax.v - s)
         arrive(us[r], v, 3 + 3 * r)
         send(ax.chunk(out, us[r], v, cols), us[r], v, ax.device(v=wrap(ax.v + s)), 5 + 3 * r)
-        yield base + 4.5 + 2.5 * r
+        yield base + GATHER_AT[2] + GATHER_AT[3] * r + 0.1
         arrive(us[r], wrap(ax.v + s), 4 + 3 * r)
-        yield base + (5 if r == 0 else 4 + 2.5 * (r + 1))
+        yield base + GATHER_AT[2] + GATHER_AT[3] * (r + 1)
     for r in range(4):
+        yield base + GATHER_AT[2] + GATHER_AT[3] * r + GATHER_AT[4]
         arrive(us[r], wrap(ax.v + 2), 5 + 3 * r)
-        yield base + 14 + r
     yield 90
     for copy in sent:
         copy.wait_send()
@@ -286,11 +291,10 @@
     yield from merge_own(place, own, other, both, sems.at[0, 0, 0, 15], sems.at[0, 0, 1, 15])
     keep = pltpu.make_async_copy(both, out.at[place.y, place.x], local)
     keep.start()
-    yield base + 2
     yield from merge(
         [
             gather_half(
-                Axes(place, h, n), both, out, base + 2,
+                Axes(place, h, n), both, out, base,
                 sems.at[h, 0, 0], sems.at[h, 0, 1], sems.at[h, 1, 0], sems.at[h, 1, 1],
             )
             for h in (0, 1)
@@ -328,8 +332,8 @@
     vs = [wrap(ax.v + 2), wrap(ax.v - s), wrap(ax.v + s), ax.v]
     for_partner = [wrap(ax.v + 2), wrap(ax.v + s), wrap(ax.v - s), ax.v]
     sent, loads, gets = [], [], []
-    yield base
     for k in range(4):
+        yield 0.1 * k
         give = remote(
             ax.group(grads, for_partner[k], ax.theirs),
             got.at[k],
@@ -343,7 +347,7 @@
         load = pltpu.make_async_copy(ax.group(grads, vs[k], ax.mine), held.at[k], sems.at[2, k])
         load.start()
         loads.append(load)
-    yield base + 3
+    yield base + SCATTER_AT[0]
 
     def chip_sum(k):
         loads[k].wait()
@@ -357,22 +361,30 @@
         return copy
 
     chip_sum(0)
-    far = send(got.at[0], b1, 4, ax.device(v=wrap(ax.v + s)))
-    yield base + 4
+    far = [
+        send(got.at[0, pl.ds(2 * i, 2)], b1.at[pl.ds(2 * i, 2)], 4 + i, ax.device(v=wrap(ax.v + s)))
+        for i in (0, 1)
+    ]
+    yield base + SCATTER_AT[1]
     chip_sum(1)
-    back = send(got.at[1], b2, 5, ax.device(v=wrap(ax.v - s)))
-    yield base + 6
+    back = send(got.at[1], b2, 6, ax.device(v=wrap(ax.v - s)))
+    yield base + SCATTER_AT[2]
     chip_sum(2)
-    yield base + 8
-    far.wait_recv()
-    add_chunks(4, lambda i: b1.at[i], lambda i: b1.at[i], lambda i: got.at[2, i])
-    forth = send(b1, b3, 6, ax.device(v=wrap(ax.v + s)))
-    yield base + 9
+    forth = []
+    for i in (0, 1):
+        yield base + SCATTER_AT[3 + i]
+        far[i].wait_recv()
+        add_chunks(2, lambda k: b1.at[2 * i + k], lambda k: b1.at[2 * i + k], lambda k: got.at[2, 2 * i + k])
+        forth.append(
+            send(b1.at[pl.ds(2 * i, 2)], b3.at[pl.ds(2 * i, 2)], 7 + i, ax.device(v=wrap(ax.v + s)))
+        )
+    yield base + SCATTER_AT[5]
     loads[3].wait()
     gets[3].wait_recv()
     back.wait_recv()
-    yield base + 13
-    forth.wait_recv()
+    yield base + SCATTER_AT[6]
+    for move in forth:
+        move.wait_recv()
     add_chunks(
         4,
         lambda i: total.at[i],
@@ -381,24 +393,24 @@
         lambda i: b2.at[i],
         lambda i: b3.at[i],
     )
-    far = send(total.at[wrap(ax.u + 2)], c1, 7, ax.device(u=wrap(ax.u + s)))
-    back = send(total.at[wrap(ax.u - s)], c2, 8, ax.device(u=wrap(ax.u - s)))
-    yield base + 17
+    far = send(total.at[wrap(ax.u + 2)], c1, 9, ax.device(u=wrap(ax.u + s)))
+    back = send(total.at[wrap(ax.u - s)], c2, 10, ax.device(u=wrap(ax.u - s)))
+    yield base + SCATTER_AT[7]
     far.wait_recv()
     add_chunks(1, lambda i: c1, lambda i: c1, lambda i: total.at[wrap(ax.u + s)])
-    forth = send(c1, c3, 9, ax.device(u=wrap(ax.u + s)))
-    yield base + 21
+    forth = send(c1, c3, 11, ax.device(u=wrap(ax.u + s)))
     back.wait_recv()
+    yield base + SCATTER_AT[8]
     forth.wait_recv()
     add_chunks(1, lambda i: c2, lambda i: total.at[ax.u], lambda i: c2, lambda i: c3)
     keep = pltpu.make_async_copy(c2, final.at[:, ax.mine], sems.at[2, 4])
     keep.start()
-    last = send(c2, final.at[:, ax.mine], 10, place.partner())
+    last = send(c2, final.at[:, ax.mine], 12, place.partner())
     yield 90
     for copy in sent:
         copy.wait_send()
     keep.wait()
-    remote(c2, final.at[:, ax.theirs], sems.at[0, 10], sems.at[1, 10], place.partner()).wait_recv()
+    remote(c2, final.at[:, ax.theirs], sems.at[0, 12], sems.at[1, 12], place.partner()).wait_recv()
 
 
 def scatter_scratch(n):
@@ -408,7 +420,7 @@
         shapes += [pltpu.VMEM((4, CHUNK, w), BF16)] * 3
         shapes += [pltpu.VMEM((CHUNK, w), BF16)] * 3
         shapes += [pltpu.VMEM((4, CHUNK, w), BF16)]
-        shapes += [pltpu.SemaphoreType.DMA((3, 11))]
+        shapes += [pltpu.SemaphoreType.DMA((3, 13))]
     return shapes
 
 
@@ -419,27 +431,34 @@
         yield scatter_half(Axes(place, h, n), grads, final, part[:9], part[9], base)
 
 
+HALVES = (pl.ds(0, 80), pl.ds(80, 80))
+
+
 def rows_gather(place, out, sems, base=0):
     s, z = place.s, place.z
     ahead, behind = place.device(z=wrap(z + s)), place.device(z=wrap(z - s))
 
-    def copy(slot, k, device):
-        return remote(out.at[slot], out.at[slot], sems.at[0, k], sems.at[1, k], device)
-
-    first = copy(z, 0, ahead)
-    first.start()
-    second = copy(z, 1, behind)
-    second.start()
-    yield base + 9
-    copy(wrap(z - s), 0, ahead).wait_recv()
-    relay = copy(wrap(z - s), 2, ahead)
-    relay.start()
-    yield base + 9.5
-    copy(wrap(z + s), 1, ahead).wait_recv()
-    yield base + 14
-    copy(wrap(z + 2), 2, ahead).wait_recv()
-    for sent in (first, second, relay):
-        sent.wait_send()
+    def copy(slot, rows, k, device):
+        here = out.at[slot, rows]
+        return remote(here, here, sems.at[0, k], sems.at[1, k], device)
+
+    sent = [copy(z, HALVES[i], i, ahead) for i in (0, 1)] + [copy(z, HALVES[i], 2 + i, behind) for i in (0, 1)]
+    for move in sent:
+        move.start()
+    for i in (0, 1):
+        yield base + ROWS_AT[i]
+        copy(wrap(z - s), HALVES[i], i, ahead).wait_recv()
+        relay = copy(wrap(z - s), HALVES[i], 4 + i, ahead)
+        relay.start()
+        sent.append(relay)
+    for i in (0, 1):
+        yield base + ROWS_AT[2]
+        copy(wrap(z + s), HALVES[i], 2 + i, ahead).wait_recv()
+    for i in (0, 1):
+        yield base + ROWS_AT[3 + i]
+        copy(wrap(z + 2), HALVES[i], 4 + i, ahead).wait_recv()
+    for move in sent:
+        move.wait_send()
 
 
 def rows_scatter(place, parts, bufs, sems):
@@ -447,35 +466,38 @@
     b1, b2, b3 = bufs
     ahead, behind = place.device(z=wrap(z + s)), place.device(z=wrap(z - s))
 
-    def copy(src, dst, k, device):
-        return remote(src, dst, sems.at[0, k], sems.at[1, k], device)
-
-    far = copy(parts.at[wrap(z + 2)], b1, 0, ahead)
-    far.start()
-    back = copy(parts.at[wrap(z - s)], b2, 1, behind)
-    back.start()
-    yield 9
-    far.wait_recv()
+    def copy(src, dst, rows, k, device):
+        return remote(src.at[rows], dst.at[rows], sems.at[0, k], sems.at[1, k], device)
+
+    far = [copy(parts.at[wrap(z + 2)], b1, HALVES[i], i, ahead) for i in (0, 1)]
+    back = [copy(parts.at[wrap(z - s)], b2, HALVES[i], 2 + i, behind) for i in (0, 1)]
+    forth = [copy(b1, b3, HALVES[i], 4 + i, ahead) for i in (0, 1)]
+    for move in far + back:
+        move.start()
     mid = wrap(z + s)
 
     def body(i, carry):
-        rows = pl.ds(pl.multiple_of(i * 32, 32), 32)
+        rows = pl.ds(pl.multiple_of(i * 16, 16), 16)
         b1[rows, :] = (b1[rows, :].astype(F32) + parts[mid, rows, :].astype(F32)).astype(BF16)
         return carry
 
-    lax.fori_loop(0, ROWS // 32, body, 0)
-    forth = copy(b1, b3, 2, ahead)
-    forth.start()
-    yield 10
-    back.wait_recv()
-    yield 15
-    forth.wait_recv()
-    for sent in (far, back, forth):
-        sent.wait_send()
+    for i in (0, 1):
+        yield ROWS_AT[i]
+        far[i].wait_recv()
+        lax.fori_loop(5 * i, 5 * i + 5, body, 0)
+        forth[i].start()
+    yield ROWS_AT[2]
+    for move in back:
+        move.wait_recv()
+    for i in (0, 1):
+        yield ROWS_AT[3 + i]
+        forth[i].wait_recv()
+    for move in far + back + forth:
+        move.wait_send()
 
 
 def rows_scratch():
-    return [pltpu.VMEM((ROWS, WIDTH), BF16)] * 3 + [pltpu.SemaphoreType.DMA((2, 3))] * 2
+    return [pltpu.VMEM((ROWS, WIDTH), BF16)] * 3 + [pltpu.SemaphoreType.DMA((2, 6))] * 2
 
 
 def row_blocks(body):
@@ -501,7 +523,7 @@
     run_streams(
         [
             gather_stream(place, attn_own, mats_out, scratch[:4]),
-            gather_stream(place, own_g, full_g, scratch[4:8], 6),
+            gather_stream(place, own_g, full_g, scratch[4:8], 0.5),
             z_stream(),
         ]
     )
@@ -526,13 +548,13 @@
             rows_out[place.z, rows, :] = (mid * gains[2:3, :]).astype(BF16)
 
         row_blocks(body)
-        yield from rows_gather(place, rows_out, sems2, 17)
+        yield from rows_gather(place, rows_out, sems2, 18)
 
     run_streams(
         [
             z_stream(),
             gather_stream(place, own_u, full_u, scratch[5:9]),
-            gather_stream(place, own_d, full_d, scratch[9:13], 9),
+            gather_stream(place, own_d, full_d, scratch[9:13], 0.5),
         ]
     )
 
@@ -561,7 +583,7 @@
             rows_out[place.z, rows, :] = normalize_back(grad * gains[3:4, :], hat, inverse).astype(BF16)
 
         row_blocks(body)
-        yield from rows_gather(place, rows_out, sems2, 17)
+        yield from rows_gather(place, rows_out, sems2, 18)
 
     held_g, held_u, moves = scratch[5:8]
 
@@ -632,11 +654,11 @@
             ).astype(BF16)
 
         row_blocks(body)
-        yield from rows_gather(place, rows_out, sems2, 17)
+        yield from rows_gather(place, rows_out, sems2, 18)
 
     streams = [z_stream()]
     for i, (grads, final) in enumerate(((grad_d, sum_d), (grad_g, sum_g))):
-        streams += list(scatter_streams(place, grads, final, scratch[5 + 20 * i : 25 + 20 * i], 9 * i))
+        streams += list(scatter_streams(place, grads, final, scratch[5 + 20 * i : 25 + 20 * i], 0.5 * i))
     run_streams(streams)
 
 
@@ -674,10 +696,10 @@
             total = total + got[k].astype(F32)
         shared[...] = total
 
-    run_streams([attn_stream(), z_stream()] + list(scatter_streams(place, grad_u, sum_u, scratch[28:48], 5)))
-
-
-def call(kernel, outs, ins, spaces, out_spaces, scratch, ident):
+    run_streams([attn_stream(), z_stream()] + list(scatter_streams(place, grad_u, sum_u, scratch[28:48], 0.5)))
+
+
+def call(kernel, outs, ins, spaces, out_spaces, scratch, ident, name=None):
     return pl.pallas_call(
         kernel,
         out_shape=[jax.ShapeDtypeStruct(shape, dtype) for shape, dtype in outs],
@@ -687,7 +709,7 @@
         compiler_params=pltpu.CompilerParams(
             collective_id=ident, has_side_effects=True, vmem_limit_bytes=60 * 1024 * 1024
         ),
-        name=kernel.__name__,
+        name=name or kernel.__name__,
     )(*ins)
 
 
@@ -717,14 +739,15 @@
     pad = ((0, 0), (0, FFPAD - hidden_units))
     width = w_key.shape[1]
 
-    def column(vector):
-        return jnp.pad(vector, (0, shard - vector.shape[0]))[:, None]
-
+    vectors = jnp.stack(
+        [
+            jnp.pad(g, (0, shard - g.shape[0]))
+            for g in (prenorm_attn, postnorm_attn, prenorm_ffw, postnorm_ffw, query_norm, key_norm)
+        ]
+    )
+    spread = jnp.eye(6, 256, dtype=BF16)
     attn_own = jnp.concatenate(
-        [w_query, w_out.T, w_key, w_value]
-        + [column(g) for g in (prenorm_attn, postnorm_attn, prenorm_ffw, postnorm_ffw, query_norm, key_norm)]
-        + [jnp.zeros((shard, ATTN_COLS - 1024 - 6), BF16)],
-        axis=1,
+        [w_query, w_out.T, w_key, w_value, contract_rows(vectors, spread).astype(BF16)], axis=1
     )
     whole = ((4, 4, CHUNK, FFPAD), BF16)
     tokens_all, mats, full_gate = call(
@@ -733,7 +756,7 @@
         [tokens, attn_own, jnp.pad(w_gate, pad)],
         [vm, vm, vm],
         [vm, hbm, hbm],
-        [pltpu.SemaphoreType.DMA((2, 3))] + gather_scratch(ATTN_COLS) + gather_scratch(FFPAD),
+        [pltpu.SemaphoreType.DMA((2, 6))] + gather_scratch(ATTN_COLS) + gather_scratch(FFPAD),
         0,
     )
     mats = mats.reshape(WIDTH, ATTN_COLS)
@@ -839,9 +862,6 @@
     grad_key_norm = jnp.sum(grad_key_turned * key_hat, axis=0)
     key_in = normalize_back(grad_key_turned * gain_key, key_hat, key_inverse).astype(BF16)
     value_in = grad_values.astype(BF16)
-    grad_query = contract_rows(attn_rows, query_in)
-    grad_key = contract_rows(attn_rows, key_in)
-    grad_value = contract_rows(attn_rows, value_in)
     in_part = contract_cols(query_in, full_query)
     in_part = in_part + contract_cols(key_in, full_key)
     in_part = in_part + contract_cols(value_in, full_value)
@@ -860,9 +880,10 @@
             placed_rows(grad_key_norm),
         ]
     )
-    small_grads = jnp.pad(vectors, ((0, ATTN_COLS - 1024 - 6), (0, 0))).T
+    small_grads = contract_rows(vectors.astype(BF16), spread)
+    grad_qkv = contract_rows(attn_rows, jnp.concatenate([query_in, key_in, value_in], axis=1))
     grads = jnp.concatenate(
-        [g.astype(BF16) for g in (grad_query, grad_output, grad_key, grad_value, small_grads)], axis=1
+        [g.astype(BF16) for g in (grad_qkv[:, :256], grad_output, grad_qkv[:, 256:], small_grads)], axis=1
     )
     grad_in_rows, sum_attn, sum_shared, sum_up = call(
         end_kernel,

time: 337 us -> 320 us (0.950)
  Pallas kernels: 213 us -> 200 us
  matrix products: 75.4 us -> 71.1 us
    pallas_call x5, Pallas kernels: 213 us -> 200 us  [call(): pl.pallas_call(kernel, out_shape=[jax.ShapeDtypeStruct(shape, dtype) for...]
    broadcast_in_dim x9 -> x0, local copies, waits for them, and re-layouts: 4.62 us -> none  [the longest x8 4.61 us: column(): return jnp.pad(vector, (0, shard - vector.shape[0]))[:, None]]
    concatenate x3 -> x1, local copies, waits for them, and re-layouts: 8.16 us -> 3.72 us  [local(): jnp.concatenate([g.astype(BF16) for g in (grad_qkv[:, :256], grad_output,...]
    unnamed x96 -> x92, local copies, waits for them, and re-layouts: 4 us -> 8.43 us
    dot_general x9, matrix products: 27.1 us -> 22.9 us  [contract_rows(): lax.dot_general(left, right, (((0,), (0,)), ((), ())), preferred_element_...]
where the time goes in v3:
time: 320 us; the launch traced here: 315 us
  Pallas kernels  200 us (62%)
  matrix products  71.1 us (22%)
  local copies, waits for them, and re-layouts  26.2 us (8%)
  other arithmetic  15.3 us (5%)
    pallas_call x5, Pallas kernels, call(): pl.pallas_call(kernel, out_shape=[jax.ShapeDtypeStruct(shape, dtype) for...  200 us
    dot_general x9, matrix products, contract_rows(): lax.dot_general(left, right, (((0,), (0,)), ((), ())), preferred_element_...  22.9 us
    dot_general x9, matrix products, contract_cols(): lax.dot_general(left, right, (((1,), (1,)), ((), ())), preferred_element_...  20.1 us
    dot_general x1, matrix products, local(): grad_act = jnp.dot(grad_ffw, full_down, preferred_element_type=F32)  8.52 us
    unnamed x92, local copies, waits for them, and re-layouts  8.43 us

profile of v3, /device:TPU:0, one launch (start us, length us, event | category | flops | bytes accessed | tf_op | source)
XLA Modules:
  0.0 314.7 jit_solution(8369610028512782733)
XLA Ops:
  0.6 0.7 pad_bitcast_fusion
  1.3 0.7 stack.47
  2.1 0.7 constant_dynamic-update-slice_fusion.2
  2.8 0.7 bitcast_dynamic-update-slice_fusion
  3.5 0.7 constant_dynamic-update-slice_fusion.1
  4.2 0.7 constant_dynamic-update-slice_fusion
  5.2 1.6 pad.28.own_g
  6.8 36.6 %start_kernel.1 = (bf16[4,160,1152]{2,1,0:T(8,128)(2,1)}, bf16[4,4,72,1280]{3,2,1,0:T(8,128)(2,1)}, bf16[4,4,72,1792]{3,2,1,0:T(8,128)(2,1)}) custom-call(bf16[160,1152]{1,0:T(8,128)(2,1)} %tokens.7, bf16[36,1280]{1,0:T(8,128)(2,1)} %copy-done.28, bf16[36,1792]{1,0:T(8,128)(2,1)} %pad.28.own_g), custom_call_target="tpu_custom_call" | custom-call | tf_op jit(solution)/shard_map/start_kernel/pallas_call | solution.py:703
  43.4 1.1 slice.201
  44.7 1.7 multiply_reduce_fusion.1
  47.0 1.1 copy-done.12
  48.0 1.8 multiply_reduce_fusion.7
  50.1 0.6 copy-done.4
  50.9 2.2 multiply_reduce_fusion.8
  53.5 2.3 fusion.60
  55.9 1.7 fusion.81
  57.9 1.7 convolution_convert_fusion.11
  59.5 0.7 copy-done.15
  60.3 0.5 convolution_convert_fusion.10
  60.7 2.8 convolution_convert_fusion.4
  63.6 0.7 pad.29.own_u
  64.2 0.7 pad.30.own_d
  64.9 39.9 %middle_kernel.1 = (bf16[4,160,1152]{2,1,0:T(8,128)(2,1)}, f32[160,1152]{1,0:T(8,128)}, bf16[4,4,72,1792]{3,2,1,0:T(8,128)(2,1)}, bf16[4,4,72,1792]{3,2,1,0:T(8,128)(2,1)}) custom-call(bf16[4,160,1152]{2,1,0:T(8,128)(2,1)} %bitcast.89, bf16[160,1152]{1,0:T(8,128)(2,1)} %tokens.7, f32[8,1152]{1,0:T(8,128)} %copy-done.18, bf16[36,1792]{1,0:T(8,128)(2,1)} %pad.29.own_u, ...), custom_call_target="tpu_custom_call" | custom-call | tf_op jit(solution)/shard_map/middle_kernel/pallas_call | solution.py:703
  104.8 5.9 %fusion.82 = f32[640,1792]{1,0:T(8,128)S(1)} fusion(bf16[640,1152]{1,0:T(8,128)(2,1)} %bitcast.121, bf16[1152,1792]{1,0:T(8,128)(2,1)} %bitcast.117), kind=kOutput, calls=%fused_computation.164 | convolution fusion | flops 2642411520 | bytes 10190848 | tf_op jit(solution)/shard_map/dot_general | solution.py:802
  110.8 4.9 %fusion.5 = (bf16[640,1792]{1,0:T(8,128)(2,1)S(1)}, f32[640,1792]{1,0:T(8,128)}) fusion(f32[640,1792]{1,0:T(8,128)S(1)} %fusion.82, bf16[640,1152]{1,0:T(8,128)(2,1)S(1)} %bitcast.123, bf16[1152,1792]{1,0:T(8,128)(2,1)S(1)} %bitcast.119), kind=kOutput, calls=%fused_computation.9 | convolution fusion | flops 2653880320 | bytes 17072128 | tf_op jit(solution)/shard_map/dot_general | solution.py:803
  115.7 4.3 %convolution_convert_fusion.5 = bf16[640,1152]{1,0:T(8,128)(2,1)} fusion(bf16[640,1792]{1,0:T(8,128)(2,1)S(1)} %get-tuple-element.104, bf16[1152,1792]{1,0:T(8,128)(2,1)S(1)} %bitcast.96), kind=kOutput, calls=%fused_computation.20 | convolution fusion | flops 2643148800 | bytes 7897088 | tf_op jit(solution)/shard_map/dot_general | solution.py:80
  120.0 35.0 %turn_kernel.1 = (bf16[4,160,1152]{2,1,0:T(8,128)(2,1)}, bf16[160,1152]{1,0:T(8,128)(2,1)}, f32[8,1152]{1,0:T(8,128)}, f32[8,80,1792]{2,1,0:T(8,128)}, f32[8,80,1792]{2,1,0:T(8,128)}) custom-call(bf16[4,160,1152]{2,1,0:T(8,128)(2,1)} %bitcast.109, bf16[160,1152]{1,0:T(8,128)(2,1)} %tokens.7, f32[160,1152]{1,0:T(8,128)} %get-tuple-element.42.attn_sum, ...), custom_call_target="tpu_custom_call" | custom-call | tf_op jit(solution)/shard_map/turn_kernel/pallas_call | solution.py:703
  155.0 8.5 %fusion.6 = (bf16[640,1792]{1,0:T(8,128)(2,1)S(1)}, bf16[640,1792]{1,0:T(8,128)(2,1)S(1)}) fusion(f32[8,80,1792]{2,1,0:T(8,128)} %get-tuple-element.46, f32[8,80,1792]{2,1,0:T(8,128)} %get-tuple-element.45, bf16[640,1152]{1,0:T(8,128)(2,1)} %bitcast.106, bf16[1152,1792]{1,0:T(8,128)(2,1)} %bitcast.95), kind=kOutput, calls=%fused_computation.11 | convolution fusion | flops 2646999040 | bytes 19365888 | tf_op jit(solution)/shard_map/dot_general | solution.py:827
  163.6 5.4 %convolution_convert_fusion.1 = bf16[1152,1792]{1,0:T(8,128)(2,1)} fusion(bf16[640,1152]{1,0:T(8,128)(2,1)S(1)} %bitcast.124, bf16[640,1792]{1,0:T(8,128)(2,1)S(1)} %get-tuple-element.73), kind=kOutput, calls=%fused_computation.1 | convolution fusion | flops 2644475904 | bytes 7897088 | tf_op jit(solution)/shard_map/dot_general | solution.py:74
  169.0 5.4 %convolution_convert_fusion.2 = bf16[1152,1792]{1,0:T(8,128)(2,1)} fusion(bf16[640,1152]{1,0:T(8,128)(2,1)S(1)} %bitcast.107, bf16[640,1792]{1,0:T(8,128)(2,1)S(1)} %copy-done.42), kind=kOutput, calls=%fused_computation.2 | convolution fusion | flops 2644475904 | bytes 7897088 | tf_op jit(solution)/shard_map/dot_general | solution.py:74
  174.4 3.2 %fusion.83 = f32[640,1152]{1,0:T(8,128)S(1)} fusion(bf16[640,1792]{1,0:T(8,128)(2,1)S(1)} %get-tuple-element.73, bf16[1152,1792]{1,0:T(8,128)(2,1)S(1)} %bitcast.118), kind=kOutput, calls=%fused_computation.165 | convolution fusion | flops 2642411520 | bytes 9371648 | tf_op jit(solution)/shard_map/dot_general | solution.py:80
  177.5 4.3 %fusion.8 = bf16[640,1152]{1,0:T(8,128)(2,1)} fusion(f32[640,1152]{1,0:T(8,128)S(1)} %fusion.83, bf16[640,1792]{1,0:T(8,128)(2,1)S(1)} %get-tuple-element.72, bf16[1152,1792]{1,0:T(8,128)(2,1)S(1)} %bitcast.120), kind=kOutput, calls=%fused_computation.19 | convolution fusion | flops 2643886080 | bytes 10846208 | tf_op jit(solution)/shard_map/dot_general | solution.py:80
  181.8 48.4 %back_kernel.1 = (bf16[4,160,1152]{2,1,0:T(8,128)(2,1)}, f32[160,1152]{1,0:T(8,128)}, f32[16,1152]{1,0:T(8,128)}, bf16[72,1792]{1,0:T(8,128)(2,1)}, bf16[72,1792]{1,0:T(8,128)(2,1)}) custom-call(bf16[4,160,1152]{2,1,0:T(8,128)(2,1)} %bitcast.108, bf16[160,1152]{1,0:T(8,128)(2,1)} %tokens.7, f32[160,1152]{1,0:T(8,128)} %get-tuple-element.42.attn_sum, ...), custom_call_target="tpu_custom_call" | custom-call | tf_op jit(solution)/shard_map/back_kernel/pallas_call | solution.py:703
  230.2 1.7 fusion.77
  231.9 1.7 convert_bitcast_fusion
  233.6 2.1 convolution_convert_fusion.9
  235.8 0.5 convolution_convert_fusion.8
  236.3 0.5 multiply_reduce_fusion.2
  237.3 0.5 copy-done.23
  238.3 0.5 fusion.70
  238.8 1.5 fusion.57
  241.1 0.8 copy-done.14
  241.9 1.6 convolution_convert_fusion.3
  243.6 1.1 slice.220
  244.7 0.7 copy-done.40
  245.4 1.5 convolution_convert_fusion.7
  246.9 0.9 slice.219
  247.8 0.6 fusion.34
  248.4 0.7 convolution_add_fusion.1
  249.1 2.2 multiply_reduce_fusion
  252.3 1.8 pad_maximum_fusion
  254.1 3.7 %copy.35 = bf16[1152,1280]{1,0:T(8,128)(2,1)} copy(bf16[1152,1280]{0,1:T(8,128)(2,1)S(1)} %pad_maximum_fusion) | data formatting | bytes 5898240 | tf_op jit(solution)/shard_map/concatenate | solution.py:885
  257.8 7.4 %convolution_convert_fusion = bf16[1152,1792]{1,0:T(8,128)(2,1)} fusion(bf16[640,1152]{1,0:T(8,128)(2,1)} %bitcast.122, bf16[640,1792]{1,0:T(8,128)(2,1)} %copy-done.8), kind=kOutput, calls=%fused_computation | convolution fusion | flops 2644475904 | bytes 7897088 | tf_op jit(solution)/shard_map/dot_general | solution.py:74
  265.3 40.6 %end_kernel.1 = (f32[160,1152]{1,0:T(8,128)}, bf16[72,1280]{1,0:T(8,128)(2,1)}, f32[72,768]{1,0:T(8,128)}, bf16[72,1792]{1,0:T(8,128)(2,1)}) custom-call(bf16[4,160,1152]{2,1,0:T(8,128)(2,1)} %bitcast.88, bf16[4,4,72,1280]{3,2,1,0:T(8,128)(2,1)} %bitcast.87, bf16[4,4,72,1792]{3,2,1,0:T(8,128)(2,1)} %bitcast.94), custom_call_target="tpu_custom_call" | custom-call | tf_op jit(solution)/shard_map/end_kernel/pallas_call | solution.py:703
  305.9 1.1 fusion.78
  307.0 0.7 fusion.71
  307.8 0.7 fusion.72
  309.0 1.2 fusion.25
  310.2 0.6 fusion.80
  310.8 0.9 select_convert_fusion
  311.7 0.6 slice_bitcast_fusion
  312.3 0.7 slice_reduce_fusion.2
  313.1 0.7 slice_reduce_fusion.9
  313.8 0.7 copy.42
  (128 shorter events, 5.1 us)
Async XLA Ops:
  5.2 1.6 copy-start.28
  43.4 3.2 %copy-start.1 = (bf16[4,160,1152]{2,1,0:T(8,128)(2,1)S(1)}, bf16[4,160,1152]{2,1,0:T(8,128)(2,1)}, u32[]{:S(2)}) copy-start(bf16[4,160,1152]{2,1,0:T(8,128)(2,1)} %get-tuple-element.36) | copy-start | bytes 4423684
  44.6 5.3 %copy-start.18 = (f32[8,1152]{1,0:T(8,128)}, f32[8,1152]{1,0:T(8,128)S(1)}, u32[]{:S(2)}) copy-start(f32[8,1152]{1,0:T(8,128)S(1)} %convert_bitcast_fusion.1.gains) | copy-start | bytes 110596
  46.9 1.1 copy-start.12
  49.9 0.9 copy-start.4
  50.8 2.6 copy-start.34
  53.1 2.8 copy-start.2
  53.1 2.7 copy-start.33
  55.8 1.7 copy-start.19
  55.8 1.7 copy-start.21
  55.9 2.0 copy-start.13
  59.5 0.7 copy-start.15
  60.2 3.3 %copy-start.29 = (bf16[36,1728]{1,0:T(8,128)(2,1)S(1)}, bf16[36,1728]{1,0:T(8,128)(2,1)}, u32[]{:S(2)}) copy-start(bf16[36,1728]{1,0:T(8,128)(2,1)} %param.26) | copy-start | bytes 373252
  60.2 4.0 %copy-start.30 = (bf16[1728,36]{0,1:T(8,128)(2,1)S(1)}, bf16[1728,36]{0,1:T(8,128)(2,1)}, u32[]{:S(2)}) copy-start(bf16[1728,36]{0,1:T(8,128)(2,1)} %param.27) | copy-start | bytes 373252
  104.8 5.9 %copy-start.36 = (bf16[4,4,72,1792]{3,2,1,0:T(8,128)(2,1)S(1)}, bf16[4,4,72,1792]{3,2,1,0:T(8,128)(2,1)}, u32[]{:S(2)}) copy-start(bf16[4,4,72,1792]{3,2,1,0:T(8,128)(2,1)} %get-tuple-element.40) | copy-start | bytes 12386308
  104.8 5.9 %copy-start.38 = (bf16[4,160,1152]{2,1,0:T(8,128)(2,1)S(1)}, bf16[4,160,1152]{2,1,0:T(8,128)(2,1)}, u32[]{:S(2)}) copy-start(bf16[4,160,1152]{2,1,0:T(8,128)(2,1)} %get-tuple-element.38) | copy-start | bytes 4423684
  110.7 5.0 %copy-start.6 = (f32[640,1792]{1,0:T(8,128)}, f32[640,1792]{1,0:T(8,128)S(1)}, u32[]{:S(2)}) copy-start(f32[640,1792]{1,0:T(8,128)S(1)} %fusion.82) | copy-start | bytes 13762564
  110.8 4.9 %copy-start.7 = (bf16[4,4,72,1792]{3,2,1,0:T(8,128)(2,1)S(1)}, bf16[4,4,72,1792]{3,2,1,0:T(8,128)(2,1)}, u32[]{:S(2)}) copy-start(bf16[4,4,72,1792]{3,2,1,0:T(8,128)(2,1)} %get-tuple-element.41) | copy-start | bytes 12386308
  115.7 4.3 %copy-start.41 = (bf16[640,1792]{1,0:T(8,128)(2,1)}, bf16[640,1792]{1,0:T(8,128)(2,1)S(1)}, u32[]{:S(2)}) copy-start(bf16[640,1792]{1,0:T(8,128)(2,1)S(1)} %get-tuple-element.104) | copy-start | bytes 6881284
  155.0 8.6 %copy-start.39 = (bf16[4,160,1152]{2,1,0:T(8,128)(2,1)S(1)}, bf16[4,160,1152]{2,1,0:T(8,128)(2,1)}, u32[]{:S(2)}) copy-start(bf16[4,160,1152]{2,1,0:T(8,128)(2,1)} %get-tuple-element.38) | copy-start | bytes 4423684
  163.6 14.0 %copy-start.8 = (bf16[640,1792]{1,0:T(8,128)(2,1)}, bf16[640,1792]{1,0:T(8,128)(2,1)S(1)}, u32[]{:S(2)}) copy-start(bf16[640,1792]{1,0:T(8,128)(2,1)S(1)} %get-tuple-element.72) | copy-start | bytes 6881284
  163.6 5.4 %copy-start.11 = (bf16[4,160,1152]{2,1,0:T(8,128)(2,1)S(1)}, bf16[4,160,1152]{2,1,0:T(8,128)(2,1)}, u32[]{:S(2)}) copy-start(bf16[4,160,1152]{2,1,0:T(8,128)(2,1)} %get-tuple-element.44) | copy-start | bytes 4423684
  163.6 5.4 %copy-start.42 = (bf16[640,1792]{1,0:T(8,128)(2,1)S(1)}, bf16[640,1792]{1,0:T(8,128)(2,1)}, u32[]{:S(2)}) copy-start(bf16[640,1792]{1,0:T(8,128)(2,1)} %copy-done.41) | copy-start | bytes 6881284
  169.0 5.4 %copy-start.35 = (bf16[4,4,72,1792]{3,2,1,0:T(8,128)(2,1)S(1)}, bf16[4,4,72,1792]{3,2,1,0:T(8,128)(2,1)}, u32[]{:S(2)}) copy-start(bf16[4,4,72,1792]{3,2,1,0:T(8,128)(2,1)} %get-tuple-element.39) | copy-start | bytes 12386308
  174.4 3.2 %copy-start.37 = (bf16[4,4,72,1792]{3,2,1,0:T(8,128)(2,1)S(1)}, bf16[4,4,72,1792]{3,2,1,0:T(8,128)(2,1)}, u32[]{:S(2)}) copy-start(bf16[4,4,72,1792]{3,2,1,0:T(8,128)(2,1)} %get-tuple-element.40) | copy-start | bytes 12386308
  233.6 2.7 copy-start.16
  236.8 0.9 copy-start.23
  236.8 1.0 copy-start.24
  236.9 1.4 copy-start.20
  236.9 1.4 copy-start.22
  238.3 2.0 copy-start.5
  238.8 1.9 copy-start.3
  240.5 1.4 copy-start.14
  243.6 1.8 copy-start.40
  245.4 2.4 copy-start.10
  249.1 2.7 copy-start.31
  249.1 2.7 copy-start.32
  265.3 42.5 %copy-start.26 = (bf16[72,1792]{1,0:T(8,128)(2,1)S(1)}, bf16[72,1792]{1,0:T(8,128)(2,1)}, u32[]{:S(2)}) copy-start(bf16[72,1792]{1,0:T(8,128)(2,1)} %get-tuple-element.54) | copy-start | bytes 774148
  305.8 2.7 copy-start
  305.8 2.9 copy-start.9
  305.8 3.1 copy-start.17
  307.8 2.4 copy-start.27
  308.7 5.1 %copy-start.25 = (bf16[160,1152]{1,0:T(8,128)(2,1)S(1)}, bf16[160,1152]{1,0:T(8,128)(2,1)}, u32[]{:S(2)}) copy-start(bf16[160,1152]{1,0:T(8,128)(2,1)} %get-tuple-element.126) | copy-start | bytes 1105924
